TPU v7x, 256 devices: a whole 4x4x8 slice. The times are simulated.
256 devices in a mesh: batch: 16 (over z, core), proto: 16 (over x, y).
Axes of the slice: x: 4, y: 4, z: 8, core: 2. Of those that a mesh axis runs over, the one named last changes fastest.
Arguments:
- slow_embed: bfloat16 [16384, 256], P('batch'), may hold values from -1 to 1
- fast_embed: bfloat16 [16384, 256], P('batch'), may hold values from -1 to 1
- prototypes: float32 [32768, 256], P('proto'), may hold values from -1 to 1
Outputs:
- proto_grad: float32 [32768, 256], P('proto')
- slow_grad: float32 [16384, 256], P('batch')
- fast_grad: float32 [16384, 256], P('batch')
All inputs are finite; a program needn't handle non-finite values.
Results may differ from a plain program's by a relative error of at most 0.0005.
The roundings to bfloat16 on the way count: a program that leaves them out, or rounds other values in their place, can miss the bound.
Values sent between devices are 32-bit elements; how exact they have to be, the bound alone decides.
A program may use at most 128 MiB of HBM per device.

v0:
```python
import jax
import jax.numpy as jnp
from jax import lax
from jax.sharding import PartitionSpec as P

ITERS = 3


CODE_EPS = 0.05
TEMPER = 0.1
NORM_EPS = 1e-06


def normalize(raw_rows):
    lengths = jnp.sqrt(jnp.sum(raw_rows * raw_rows, axis=-1, keepdims=True) + 1e-12)
    return (raw_rows / lengths, lengths)


def project_back(grad_unit, unit_vec, lengths):
    along = jnp.sum(unit_vec * grad_unit, axis=-1, keepdims=True)
    return (grad_unit - unit_vec * along) / lengths


def row_total(row_terms):
    return lax.psum(row_terms, "proto")


def normalizers(proto_square, embed_square, proto_entries, embed_entries):
    totals = lax.psum((proto_square, embed_square), ("batch", "proto"))
    proto_factor = lax.rsqrt(totals[0] / proto_entries + NORM_EPS)
    embed_factor = lax.rsqrt(totals[1] / embed_entries + NORM_EPS)
    return (proto_factor, embed_factor)


def body(slow_embed, fast_embed, prototypes):
    clip_dev = slow_embed.shape[0]
    proto_dev = prototypes.shape[0]
    feat_width = prototypes.shape[1]
    batch_count = lax.axis_size("batch")
    proto_count = lax.axis_size("proto")
    clips_all = clip_dev * batch_count
    protos_all = proto_dev * proto_count
    proto_entries = float(protos_all * feat_width)
    embed_entries = float(2 * clips_all * feat_width)
    raw_views = jnp.stack([slow_embed, fast_embed]).astype(jnp.float32)
    unit_vec, lengths = normalize(raw_views)
    unit_b = unit_vec.astype(jnp.bfloat16)
    proto_unit, proto_len = normalize(prototypes)
    proto_b = proto_unit.astype(jnp.bfloat16)
    scores = jnp.einsum("vbd,kd->vbk", unit_b, proto_b, preferred_element_type=jnp.float32)
    code_table = jnp.exp(scores / CODE_EPS)
    soft_exp = jnp.exp(scores / TEMPER)
    denom_terms = jnp.sum(soft_exp, axis=2)
    denominator = lax.psum(denom_terms, "proto")
    clip_scale = jnp.ones((2, clip_dev), jnp.float32)
    for iteration in range(ITERS):
        col_total = lax.psum(jnp.sum(code_table * clip_scale[:, :, None], axis=1), "batch")
        proto_scale = 1.0 / (protos_all * col_total)
        row_terms = jnp.sum(code_table * proto_scale[:, None, :], axis=2)
        if iteration == 0:
            clip_total = row_total(row_terms)
        else:
            clip_total = row_total(row_terms)
        clip_scale = 1.0 / (clips_all * clip_total)
    codes = code_table * proto_scale[:, None, :] / clip_total[:, :, None]
    probs = soft_exp / denominator[:, :, None]
    score_grad = (jnp.stack([probs[0] - codes[1], probs[1] - codes[0]]) / TEMPER).astype(
        jnp.bfloat16
    )
    proto_terms = jnp.einsum("vbk,vbd->kd", score_grad, unit_b, preferred_element_type=jnp.float32)
    grad_proto_unit = lax.psum(proto_terms, "batch")
    embed_terms = jnp.einsum("vbk,kd->vbd", score_grad, proto_b, preferred_element_type=jnp.float32)
    grad_unit = lax.psum(embed_terms, "proto")
    grad_proto = project_back(grad_proto_unit, proto_unit, proto_len)
    grad_embed = project_back(grad_unit, unit_vec, lengths)
    proto_factor, embed_factor = normalizers(
        jnp.sum(grad_proto * grad_proto) / batch_count,
        jnp.sum(grad_embed * grad_embed) / proto_count,
        proto_entries,
        embed_entries,
    )
    proto_grad = grad_proto * proto_factor
    slow_grad = grad_embed[0] * embed_factor
    fast_grad = grad_embed[1] * embed_factor
    return (proto_grad, slow_grad, fast_grad)


def solution(mesh):
    placed = (P("batch", None), P("batch", None), P("proto", None))
    return jax.shard_map(
        body,
        mesh=mesh,
        in_specs=placed,
        out_specs=(P("proto", None), P("batch", None), P("batch", None)),
        check_vma=False,
    )
```

profile of v0, /device:TPU:1, one launch (start us, length us, event | category | flops | bytes accessed | tf_op | source)
XLA Modules:
  0.0 716.6 jit_solution(129335976540485152)
XLA Ops:
  7.2 0.0 all-reduce.5.cloned.1.call-start
  7.2 1.6 fusion.5
  8.8 1.9 multiply_reduce_fusion.9
  10.7 9.2 %fusion.4 = (f32[2,2048]{1,0:T(2,128)S(1)}, f32[2,1024,2048]{2,1,0:T(8,128)}) fusion(f32[2048,256]{1,0:T(8,128)} %param.5, f32[2048]{0:T(1024)S(1)} %add_sqrt_fusion, f32[2,1024]{1,0:T(2,128)S(1)} %add_sqrt_fusion.1, bf16[1,1024,256]{2,1,0:T(8,128)(2,1)} %bitcast.16, bf16[1,1024,256]{2,1,0:T(8,128)(2,1)} %bitcast.20), kind=kOutput, calls=%fused_computation.15 | convolution fusion | flops 2159013888 | bytes 19955712 | tf_op jit(solution)/shard_map/vbd,kd->vbk/dot_general | solution.py:50
  20.0 48.8 %psum.78 = f32[2,2048]{1,0:T(2,128)S(1)} all-reduce(f32[2,2048]{1,0:T(2,128)S(1)} %get-tuple-element.17), channel_id=1, replica_groups=mesh['batch'=16,'proto'=16] {'batch'}, use_global_device_ids=true, to_apply=%region_5.0 | all-reduce | flops 4096 | bytes 32768 | tf_op jit(solution)/shard_map/psum | solution.py:57
  68.8 9.0 %fusion.3 = (f32[2,1024]{1,0:T(2,128)S(1)}, f32[2,1024]{1,0:T(2,128)S(1)}) fusion(f32[2,1024,2048]{2,1,0:T(8,128)} %get-tuple-element.18, f32[2,2048]{1,0:T(2,128)S(1)} %multiply_divide_fusion.3), kind=kLoop, calls=%fused_computation.12 | loop fusion | flops 20967424 | bytes 16809984 | tf_op jit(solution)/shard_map/reduce_sum | solution.py:53
  77.8 34.0 %psum.79 = f32[2,1024]{1,0:T(2,128)S(1)} all-reduce(f32[2,1024]{1,0:T(2,128)S(1)} %get-tuple-element.4), channel_id=1, replica_groups=mesh['batch'=16,'proto'=16] {'proto'}, use_global_device_ids=true, to_apply=%region_7.0 | all-reduce | flops 2048 | bytes 16384 | tf_op jit(solution)/shard_map/psum | solution.py:25
  111.8 7.4 %multiply_reduce_fusion.2 = f32[2,2048]{1,0:T(2,128)S(1)} fusion(f32[2,1024]{1,0:T(2,128)S(1)} %multiply_divide_fusion.5, f32[2,1024,2048]{2,1,0:T(8,128)} %get-tuple-element.18), kind=kLoop, calls=%fused_computation.5 | loop fusion | flops 12578816 | bytes 16801792 | tf_op jit(solution)/shard_map/reduce_sum | solution.py:57
  119.1 52.9 %psum.80 = f32[2,2048]{1,0:T(2,128)S(1)} all-reduce(f32[2,2048]{1,0:T(2,128)S(1)} %multiply_reduce_fusion.2), channel_id=1, replica_groups=mesh['batch'=16,'proto'=16] {'batch'}, use_global_device_ids=true, to_apply=%region_9.0 | all-reduce | flops 4096 | bytes 32768 | tf_op jit(solution)/shard_map/psum | solution.py:57
  172.0 8.6 %multiply_reduce_fusion.1 = f32[2,1024]{1,0:T(2,128)S(1)} fusion(f32[2,2048]{1,0:T(2,128)S(1)} %multiply_divide_fusion.2, f32[2,1024,2048]{2,1,0:T(8,128)} %get-tuple-element.18), kind=kLoop, calls=%fused_computation.4 | loop fusion | flops 12580864 | bytes 16801792 | tf_op jit(solution)/shard_map/reduce_sum | solution.py:59
  180.6 29.0 %psum.81 = f32[2,1024]{1,0:T(2,128)S(1)} all-reduce(f32[2,1024]{1,0:T(2,128)S(1)} %multiply_reduce_fusion.1), channel_id=1, replica_groups=mesh['batch'=16,'proto'=16] {'proto'}, use_global_device_ids=true, to_apply=%region_11.0 | all-reduce | flops 2048 | bytes 16384 | tf_op jit(solution)/shard_map/psum | solution.py:25
  209.7 7.4 %multiply_reduce_fusion = f32[2,2048]{1,0:T(2,128)S(1)} fusion(f32[2,1024]{1,0:T(2,128)S(1)} %multiply_divide_fusion.4, f32[2,1024,2048]{2,1,0:T(8,128)} %get-tuple-element.18), kind=kLoop, calls=%fused_computation.3 | loop fusion | flops 12578816 | bytes 16801792 | tf_op jit(solution)/shard_map/reduce_sum | solution.py:57
  217.0 52.8 %psum.82 = f32[2,2048]{1,0:T(2,128)S(1)} all-reduce(f32[2,2048]{1,0:T(2,128)S(1)} %multiply_reduce_fusion), channel_id=1, replica_groups=mesh['batch'=16,'proto'=16] {'batch'}, use_global_device_ids=true, to_apply=%region_13.0 | all-reduce | flops 4096 | bytes 32768 | tf_op jit(solution)/shard_map/psum | solution.py:57
  269.9 8.6 %multiply_reduce_fusion.4 = f32[2,1024]{1,0:T(2,128)S(1)} fusion(f32[2,2048]{1,0:T(2,128)S(1)} %multiply_divide_fusion.1, f32[2,1024,2048]{2,1,0:T(8,128)} %get-tuple-element.18), kind=kLoop, calls=%fused_computation.10 | loop fusion | flops 12580864 | bytes 16801792 | tf_op jit(solution)/shard_map/reduce_sum | solution.py:59
  278.5 57.5 %all-reduce.1 = (f32[2,1024]{1,0:T(2,128)S(1)}, f32[2,1024]{1,0:T(2,128)S(1)}) all-reduce(f32[2,1024]{1,0:T(2,128)S(1)} %multiply_reduce_fusion.4, f32[2,1024]{1,0:T(2,128)S(1)} %get-tuple-element.3), channel_id=1, replica_groups=mesh['batch'=16,'proto'=16] {'proto'}, use_global_device_ids=true, to_apply=%region_15.0 | all-reduce | flops 4096 | bytes 32768 | tf_op jit(solution)/shard_map/psum | solution.py:25
  336.0 18.3 %fusion.2 = (f32[2,1024,2048]{2,1,0:T(8,128)}, f32[2,1024,2048]{2,1,0:T(8,128)}) fusion(f32[2,1024,2048]{2,1,0:T(8,128)} %get-tuple-element.18, f32[2,1024]{1,0:T(2,128)S(1)} %get-tuple-element.8, f32[2,1024]{1,0:T(2,128)S(1)} %get-tuple-element.7, f32[2,2048]{1,0:T(2,128)S(1)} %multiply_divide_fusion.1), kind=kLoop, calls=%fused_computation.11 | loop fusion | flops 20971520 | bytes 50364416 | tf_op jit(solution)/shard_map/div | solution.py:66
  354.3 19.2 %slice_subtract_fusion.1 = (f32[1,1024,2048]{2,1,0:T(8,128)}, f32[1,1024,2048]{2,1,0:T(8,128)}) fusion(f32[2,1024,2048]{2,1,0:T(8,128)} %get-tuple-element.14, f32[2,1024,2048]{2,1,0:T(8,128)} %get-tuple-element.13), kind=kLoop, calls=%fused_computation.14 | loop fusion | flops 4194304 | bytes 50331648 | tf_op jit(solution)/shard_map/sub | solution.py:67
  373.5 0.0 copy-start
  373.5 8.8 %convolution_bitcast_fusion = f32[2048,256]{1,0:T(8,128)} fusion(f32[1,1024,2048]{2,1,0:T(8,128)} %get-tuple-element.12, f32[1,1024,2048]{2,1,0:T(8,128)} %get-tuple-element.11, f32[2,1024]{1,0:T(2,128)S(1)} %add_sqrt_fusion.1, bf16[1,1024,256]{2,1,0:T(8,128)(2,1)S(1)} %bitcast.17, bf16[1,1024,256]{2,1,0:T(8,128)(2,1)S(1)} %bitcast.21), kind=kOutput, calls=%fused_computation.16 | convolution fusion | flops 2162163712 | bytes 19931136 | tf_op jit(solution)/shard_map/vbk,vbd->kd/dot_general | solution.py:70
  382.3 0.0 all-reduce.5.cloned.1.call-update
  382.3 0.3 all-reduce.7.cloned.1.call-start
  382.6 8.5 %fusion.11 = f32[2,1024,256]{2,1,0:T(8,128)} fusion(f32[1,1024,2048]{2,1,0:T(8,128)} %get-tuple-element.12, f32[1,1024,2048]{2,1,0:T(8,128)} %get-tuple-element.11, f32[2048,256]{1,0:T(8,128)S(1)} %copy-done, f32[2048]{0:T(1024)S(1)} %add_sqrt_fusion), kind=kOutput, calls=%fused_computation.33 | convolution fusion | flops 2161115136 | bytes 20979712 | tf_op jit(solution)/shard_map/vbk,kd->vbd/dot_general | solution.py:72
  391.1 0.0 all-reduce.7.cloned.1.call-update
  391.2 116.1 %all-reduce.5.cloned.1.call-done = f32[2048,256]{1,0:T(8,128)} async-done(((f32[2048,256]{1,0:T(8,128)}), f32[2048,256]{1,0:T(8,128)}) %all-reduce.5.cloned.1.call-update) | async-done | bytes 2097168 | tf_op jit(solution)/shard_map/psum | solution.py:71
  507.3 2.2 multiply_reduce_fusion.8
  509.5 3.6 multiply_reduce_fusion.7
  513.8 0.0 copy-start.1
  513.8 97.2 %all-reduce.7.cloned.1.call-done = f32[2,1024,256]{2,1,0:T(8,128)} async-done(((f32[2,1024,256]{2,1,0:T(8,128)}), f32[2,1024,256]{2,1,0:T(8,128)}) %all-reduce.7.cloned.1.call-update) | async-done | bytes 2097168 | tf_op jit(solution)/shard_map/psum | solution.py:73
  611.0 15.5 %multiply_reduce_fusion.5 = (f32[]{:T(128)}, f32[2,1024,256]{2,1,0:T(8,128)}) fusion(f32[2,1024,256]{2,1,0:T(8,128)} %all-reduce.7.cloned.1.call-done, f32[2,1024]{1,0:T(2,128)S(1)} %add_sqrt_fusion.1, bf16[1,1024,256]{2,1,0:T(8,128)(2,1)S(1)} %bitcast.18, bf16[1,1024,256]{2,1,0:T(8,128)(2,1)S(1)} %bitcast.22), kind=kOutput, calls=%fused_computation.20 | output fusion | flops 7342334 | bytes 5251076 | tf_op jit(solution)/shard_map/mul | solution.py:21
  627.1 76.8 %all-reduce = (f32[]{:T(128)}, f32[]{:T(128)}) all-reduce(f32[]{:T(128)S(6)} %div.101, f32[]{:T(128)S(6)} %div.104), channel_id=1, replica_groups=mesh['batch'=16,'proto'=16] {'batch','proto'}, use_global_device_ids=true, to_apply=%region_19.0 | all-reduce | flops 2 | bytes 16 | tf_op jit(solution)/shard_map/psum | solution.py:29
  705.3 1.5 broadcast_multiply_fusion
  706.8 3.0 fusion.9
  (13 shorter events, 0.1 us)
Async XLA Ops:
  7.2 500.1 %all-reduce.5.cloned.1.call-start = ((), (), s32[]{:S(2)}) async-start(), calls=%async_computation | async-start | bytes 4194304 | tf_op jit(solution)/shard_map/psum | solution.py:71
  354.3 19.2 %copy-start.2 = (bf16[1024,256]{1,0:T(8,128)(2,1)S(1)}, bf16[1024,256]{1,0:T(8,128)(2,1)}, u32[]{:S(2)}) copy-start(bf16[1024,256]{1,0:T(8,128)(2,1)} %param.4) | copy-start | bytes 1572868
  354.3 19.2 %copy-start.3 = (bf16[1024,256]{1,0:T(8,128)(2,1)S(1)}, bf16[1024,256]{1,0:T(8,128)(2,1)}, u32[]{:S(2)}) copy-start(bf16[1024,256]{1,0:T(8,128)(2,1)} %param.3) | copy-start | bytes 1572868
  373.5 9.1 %copy-start = (f32[2048,256]{1,0:T(8,128)S(1)}, f32[2048,256]{1,0:T(8,128)}, u32[]{:S(2)}) copy-start(f32[2048,256]{1,0:T(8,128)} %param.5) | copy-start | bytes 6291460
  382.3 228.7 %all-reduce.7.cloned.1.call-start = ((), (), s32[]{:S(2)}) async-start(), calls=%async_computation.1 | async-start | bytes 4194304 | tf_op jit(solution)/shard_map/psum | solution.py:73
  513.8 191.5 %copy-start.1 = (f32[2048,256]{1,0:T(8,128)S(1)}, f32[2048,256]{1,0:T(8,128)}, u32[]{:S(2)}) copy-start(f32[2048,256]{1,0:T(8,128)} %get-tuple-element.10) | copy-start | bytes 6291460
Sparse Core Ops, SparseCore 0:
  382.4 124.8 all-reduce.4
  510.6 100.3 all-reduce.6
where the time goes:
time: 717 us
  blocking collectives  352 us (49%)
  waiting for transfers between devices  213 us (30%)
  other arithmetic  108 us (15%)
  matrix products  26.5 us (4%)
  between operations  16.9 us (2%)
    psum x3, blocking collectives, body(): lax.psum(jnp.sum(code_table * clip_scale[:, :, None], axis=1), 'batch')  155 us
    psum x3, blocking collectives, row_total(): return lax.psum(row_terms, 'proto')  121 us
    psum x1, waiting for transfers between devices, body(): grad_proto_unit = lax.psum(proto_terms, 'batch')  116 us
    psum x1, waiting for transfers between devices, body(): grad_unit = lax.psum(embed_terms, 'proto')  97.2 us
    psum x1, blocking collectives, normalizers(): totals = lax.psum((proto_square, embed_square), ('batch', 'proto'))  76.8 us
    sub x1, other arithmetic, body(): probs[0] - codes[1]  19.2 us
    div x1, other arithmetic, body(): probs = soft_exp / denominator[:, :, None]  18.3 us
    reduce_sum x2, other arithmetic, body(): row_terms = jnp.sum(code_table * proto_scale[:, None, :], axis=2)  17.2 us
  transfers between devices with their start and end apart: 2, of which 2 were waited for; matrix products, arithmetic and copies ran while one was open for 2% of the time, Pallas kernels for 0%

commit v1 on v0

v1 whole, which is shorter than its diff:
```python
import functools

import jax
import jax.numpy as jnp
from jax import lax
from jax.experimental import pallas as pl
from jax.experimental.pallas import tpu as pltpu
from jax.sharding import PartitionSpec as P

ITERS = 3
NORM_EPS = 1e-06
MESH = pl.DeviceIdType.MESH
F32 = jnp.float32
BF16 = jnp.bfloat16


def normalized(rows):
    total = jnp.sum(rows * rows, axis=-1, keepdims=True) + 1e-12
    inverse = 1.0 / jnp.sqrt(total)
    return rows * inverse, inverse


def fold8(block):
    rows, lanes = block.shape
    return jnp.sum(block.reshape(rows // 8, 8, lanes), axis=0)


def kernel(
    dims,
    slow_ref, fast_ref, proto_ref,
    dw_ref, dx_ref, sum_ref,
    table, grads, unit_b, unit_t, proto_b, partial, clip_b, soft_b, code_b,
    du, dct, dc_pair, dc_half, du_recv, dc_recv,
    col_z, col_pair, row_recv, den_recv, sq_p, sq_z, sq_pair, own_dx, own_dw,
    send_sem, pair_send, col_sem, colp_sem, row_sem, den_sem, den_send,
    du_sem, dcp_sem, dc_sem, sqp_sem, sqz_sem, sqr_sem, agx_sem, agw_sem, agwp_sem,
    du_send, dc_send, agx_send, agw_send, agwp_send, local_sem,
):
    clips, protos, width, n_z, n_p = dims
    batch_me = lax.axis_index("batch")
    me_p = lax.axis_index("proto")
    me_z = batch_me // 2
    core = batch_me % 2
    clips_all = clips * 2 * n_z
    protos_all = protos * n_p
    rows = 2 * clips
    lane_chunks = protos // 128
    row_blocks = rows // 128
    view_blocks = clips // 128
    embeds = (slow_ref, fast_ref)

    def p_id(d):
        return {"proto": (me_p + d) % n_p}

    def z_id(d):
        return {"batch": ((me_z + d) % n_z) * 2 + core}

    partner = {"batch": me_z * 2 + 1 - core}

    def remote(src, dst, send, recv, device):
        return pltpu.make_async_remote_copy(
            src_ref=src, dst_ref=dst, send_sem=send, recv_sem=recv,
            device_id=device, device_id_type=MESH,
        )

    barrier = pltpu.get_barrier_semaphore()
    for d in range(1, n_p):
        pl.semaphore_signal(barrier, inc=1, device_id=p_id(d), device_id_type=MESH)
    for d in range(1, n_z):
        pl.semaphore_signal(barrier, inc=1, device_id=z_id(d), device_id_type=MESH)
    pl.semaphore_signal(barrier, inc=1, device_id=partner, device_id_type=MESH)

    def proto_norm(i, carry):
        at = pl.ds(pl.multiple_of(i * 128, 128), 128)
        unit, _ = normalized(proto_ref[at, :])
        proto_b[at, :] = unit.astype(BF16)
        return carry

    lax.fori_loop(0, protos // 128, proto_norm, 0)

    def chunk(c):
        return slice(c * 128, (c + 1) * 128)

    step_w = 512
    for v in range(2):
        def first(i, cols):
            at = pl.ds(pl.multiple_of(i * 128, 128), 128)
            glob = pl.ds(pl.multiple_of(v * clips + i * 128, 128), 128)
            unit, _ = normalized(embeds[v][at, :].astype(F32))
            ub = unit.astype(BF16)
            unit_b[glob, :] = ub
            den = jnp.zeros((128, 128), F32)
            cols = list(cols)
            for k in range(protos // step_w):
                score = lax.dot_general(
                    ub, proto_b[k * step_w:(k + 1) * step_w, :],
                    (((1,), (1,)), ((), ())), preferred_element_type=F32)
                soft = jnp.exp(score * 10.0)
                table[glob, k * step_w:(k + 1) * step_w] = soft
                for j in range(step_w // 128):
                    t = soft[:, chunk(j)]
                    den = den + t
                    c = k * (step_w // 128) + j
                    cols[c] = cols[c] + fold8(t * t)
            partial[glob, :] = den
            return tuple(cols)

        cols = lax.fori_loop(
            0, view_blocks, first,
            tuple(jnp.zeros((8, 128), F32) for _ in range(lane_chunks)))
        for c in range(lane_chunks):
            col_z[0, me_z, v * lane_chunks + c:v * lane_chunks + c + 1, :] = jnp.sum(
                cols[c], axis=0, keepdims=True)

    pl.semaphore_wait(barrier, n_p - 1 + n_z - 1 + 1)

    ones = jnp.ones((8, 128), F32)

    def dense_rows(store):
        for v in range(2):
            total = lax.dot_general(
                ones, partial[v * clips:(v + 1) * clips, :], (((1,), (1,)), ((), ())),
                precision=lax.Precision.HIGHEST, preferred_element_type=F32)
            for i in range(view_blocks):
                store(v * view_blocks + i, total[0:1, chunk(i)])

    def spread(values, target):
        for i in range(row_blocks):
            target[chunk(i), :] = jnp.broadcast_to(values[i:i + 1, :], (128, 128)).T

    def start_all(ref, me, count, ids, send, recv):
        copies = []
        for d in range(1, count):
            copy = remote(ref.at[me], ref.at[me], send.at[d], recv.at[d], ids(d))
            copy.start()
            copies.append(copy)
        return copies

    def total_of(ref, count):
        acc = ref[0]
        for i in range(1, count):
            acc = acc + ref[i]
        return acc

    def col_total(it):
        buf = col_z.at[it]
        for copy in start_all(buf, me_z, n_z, z_id, send_sem, col_sem.at[it]):
            copy.wait()
        pair = col_pair.at[it]
        pair[core] = total_of(buf, n_z)
        copy = remote(pair.at[core], pair.at[core], pair_send, colp_sem.at[it], partner)
        copy.start()
        copy.wait()
        return pair[0] + pair[1]

    def row_total(it):
        buf = row_recv.at[it]

        def put(i, value):
            buf[me_p, i:i + 1, :] = value

        dense_rows(put)
        for copy in start_all(buf, me_p, n_p, p_id, send_sem, row_sem.at[it]):
            copy.wait()
        return total_of(buf, n_p)

    def put_den(i, value):
        den_recv[me_p, i:i + 1, :] = value

    dense_rows(put_den)
    den_copies = start_all(den_recv, me_p, n_p, p_id, den_send, den_sem)

    scale = None
    for it in range(ITERS):
        if it > 0:
            for v in range(2):
                def cols_pass(i, cols):
                    at = pl.ds(pl.multiple_of(v * clips + i * 64, 64), 64)
                    s = clip_b[at, :]
                    out = []
                    for c in range(lane_chunks):
                        t = table[at, chunk(c)]
                        out.append(cols[c] + fold8(t * t * s))
                    return tuple(out)

                cols = lax.fori_loop(
                    0, clips // 64, cols_pass,
                    tuple(jnp.zeros((8, 128), F32) for _ in range(lane_chunks)))
                for c in range(lane_chunks):
                    col_z[it, me_z, v * lane_chunks + c:v * lane_chunks + c + 1, :] = jnp.sum(
                        cols[c], axis=0, keepdims=True)
        scale = 1.0 / (protos_all * col_total(it))
        for v in range(2):
            def rows_pass(i, carry):
                at = pl.ds(pl.multiple_of(v * clips + i * 64, 64), 64)
                acc = jnp.zeros((64, 128), F32)
                for c in range(lane_chunks):
                    t = table[at, chunk(c)]
                    r = scale[v * lane_chunks + c:v * lane_chunks + c + 1, :]
                    acc = acc + t * t * r
                partial[at, :] = acc
                return carry

            lax.fori_loop(0, clips // 64, rows_pass, 0)
        row_sum = row_total(it)
        if it < ITERS - 1:
            spread(1.0 / (clips_all * row_sum), clip_b)
    for copy in den_copies:
        copy.wait()
    spread(10.0 / total_of(den_recv, n_p), soft_b)
    spread(10.0 / row_sum, code_b)

    for v in range(2):
        w = 1 - v

        def grad_pass(i, carry):
            mine = pl.ds(pl.multiple_of(v * clips + i * 64, 64), 64)
            other = pl.ds(pl.multiple_of(w * clips + i * 64, 64), 64)
            soft_scale = soft_b[mine, :]
            code_scale = code_b[other, :]
            for c in range(lane_chunks):
                r = scale[w * lane_chunks + c:w * lane_chunks + c + 1, :]
                t = table[other, chunk(c)]
                g = table[mine, chunk(c)] * soft_scale - t * t * r * code_scale
                grads[mine, chunk(c)] = g.astype(BF16)
            return carry

        lax.fori_loop(0, clips // 64, grad_pass, 0)

    def transpose_unit(i, carry):
        at = pl.ds(pl.multiple_of(i * 128, 128), 128)
        unit_t[:, at] = unit_b[at, :].astype(F32).T.astype(BF16)
        return carry

    lax.fori_loop(0, row_blocks, transpose_unit, 0)

    def dc_dot(i, carry):
        at = pl.ds(pl.multiple_of(i * 256, 256), 256)
        out = jnp.dot(unit_t[...], grads[:, at], preferred_element_type=F32)
        dct[2 * i] = out[:, :128]
        dct[2 * i + 1] = out[:, 128:]
        return carry

    lax.fori_loop(0, protos // 256, dc_dot, 0)
    half = pl.ds((1 - core) * n_z, n_z)
    pair_copy = remote(dct.at[half], dc_pair, pair_send, dcp_sem, partner)
    pair_copy.start()

    def du_dot(i, carry):
        at = pl.ds(pl.multiple_of(i * 256, 256), 256)
        out = jnp.dot(grads[at, :], proto_b[...], preferred_element_type=F32)
        du[2 * i] = out[:128, :]
        du[2 * i + 1] = out[128:, :]
        return carry

    lax.fori_loop(0, rows // 256, du_dot, 0)
    du_copies = []
    for d in range(1, n_p):
        copy = remote(du.at[(me_p + d) % n_p], du_recv.at[me_p], du_send.at[d], du_sem.at[d], p_id(d))
        copy.start()
        du_copies.append(copy)

    pair_copy.wait()
    for i in range(n_z):
        dc_half[i] = dct[core * n_z + i] + dc_pair[i]
    dc_copies = []
    for d in range(1, n_z):
        copy = remote(dc_half.at[(me_z + d) % n_z], dc_recv.at[me_z], dc_send.at[d], dc_sem.at[d], z_id(d))
        copy.start()
        dc_copies.append(copy)

    def project(grad, raw):
        unit, inverse = normalized(raw)
        along = jnp.sum(unit * grad, axis=-1, keepdims=True)
        return (grad - unit * along) * inverse

    def lanes_square(block):
        sq = block * block
        return jnp.sum(sq[:, :128] + sq[:, 128:], axis=0, keepdims=True)

    du_recv[me_p] = du[me_p]
    for copy in du_copies:
        copy.wait()
    total = total_of(du_recv, n_p)
    at = pl.ds(pl.multiple_of((me_p % view_blocks) * 128, 128), 128)
    is_slow = me_p < view_blocks
    raw = jnp.where(is_slow, slow_ref[at, :].astype(F32), fast_ref[at, :].astype(F32))
    dx_own = project(total, raw)
    own_dx[...] = dx_own
    agx = []
    spot = dx_ref.at[pl.ds(pl.multiple_of(me_p * 128, 128), 128), :]
    for d in range(1, n_p):
        copy = remote(own_dx, spot, agx_send.at[d], agx_sem.at[d], p_id(d))
        copy.start()
        agx.append(copy)
    local_x = pltpu.make_async_copy(own_dx, spot, local_sem.at[0])
    local_x.start()

    dc_recv[me_z] = dc_half[me_z]
    for copy in dc_copies:
        copy.wait()
    total = total_of(dc_recv, n_z).T
    at = pl.ds(pl.multiple_of((core * n_z + me_z) * 128, 128), 128)
    dw_own = project(total, proto_ref[at, :])
    own_dw[...] = dw_own
    agw = []
    spot_w = dw_ref.at[at, :]
    for d in range(1, n_z):
        copy = remote(own_dw, spot_w, agw_send.at[d], agw_sem.at[d], z_id(d))
        copy.start()
        agw.append(copy)
    local_w = pltpu.make_async_copy(own_dw, spot_w, local_sem.at[1])
    local_w.start()

    sq_p[me_p, 0:1, :] = lanes_square(dw_own)
    sq_p[me_p, 1:2, :] = lanes_square(dx_own)
    sq_p[me_p, 2:8, :] = jnp.zeros((6, 128), F32)
    for copy in start_all(sq_p, me_p, n_p, p_id, send_sem, sqp_sem):
        copy.wait()
    sq_z[me_z] = total_of(sq_p, n_p)
    for copy in start_all(sq_z, me_z, n_z, z_id, send_sem, sqz_sem):
        copy.wait()
    sq_pair[core] = total_of(sq_z, n_z)
    copy = remote(sq_pair.at[core], sq_pair.at[core], pair_send, sqr_sem, partner)
    copy.start()
    copy.wait()
    sum_ref[...] = sq_pair[0] + sq_pair[1]

    for copy in agw:
        copy.wait()
    local_w.wait()
    half_rows = pl.ds(pl.multiple_of(core * n_z * 128, 128), n_z * 128)
    copy = remote(dw_ref.at[half_rows, :], dw_ref.at[half_rows, :], agwp_send, agwp_sem, partner)
    copy.start()
    copy.wait()
    local_x.wait()
    for copy in agx:
        copy.wait()


def body(slow_embed, fast_embed, prototypes):
    clips, width = slow_embed.shape
    protos = prototypes.shape[0]
    n_b = lax.axis_size("batch")
    n_p = lax.axis_size("proto")
    n_z = n_b // 2
    rows = 2 * clips
    DMA = pltpu.SemaphoreType.DMA
    vmem = pltpu.VMEM
    lane_chunks = protos // 128
    row_blocks = rows // 128
    scratch = [
        vmem((rows, protos), F32),
        vmem((rows, protos), BF16),
        vmem((rows, width), BF16),
        vmem((width, rows), BF16),
        vmem((protos, width), BF16),
        vmem((rows, 128), F32),
        vmem((rows, 128), F32),
        vmem((rows, 128), F32),
        vmem((rows, 128), F32),
        vmem((n_p, rows // n_p, width), F32),
        vmem((lane_chunks, width, 128), F32),
        vmem((n_z, width, 128), F32),
        vmem((n_z, width, 128), F32),
        vmem((n_p, rows // n_p, width), F32),
        vmem((n_z, width, 128), F32),
        vmem((ITERS, n_z, 2 * lane_chunks, 128), F32),
        vmem((ITERS, 2, 2 * lane_chunks, 128), F32),
        vmem((ITERS, n_p, row_blocks, 128), F32),
        vmem((n_p, row_blocks, 128), F32),
        vmem((n_p, 8, 128), F32),
        vmem((n_z, 8, 128), F32),
        vmem((2, 8, 128), F32),
        vmem((rows // n_p, width), F32),
        vmem((128, width), F32),
        DMA((16,)), DMA(()), DMA((ITERS, n_z)), DMA((ITERS,)), DMA((ITERS, n_p)),
        DMA((n_p,)), DMA((n_p,)),
        DMA((n_p,)), DMA(()), DMA((n_z,)), DMA((n_p,)), DMA((n_z,)), DMA(()),
        DMA((n_p,)), DMA((n_z,)), DMA(()),
        DMA((n_p,)), DMA((n_z,)), DMA((n_p,)), DMA((n_z,)), DMA(()), DMA((2,)),
    ]
    whole = pl.BlockSpec(memory_space=pltpu.VMEM)
    anywhere = pl.BlockSpec(memory_space=pl.ANY)
    dw, dx, sums = pl.pallas_call(
        functools.partial(kernel, (clips, protos, width, n_z, n_p)),
        out_shape=(
            jax.ShapeDtypeStruct((protos, width), F32),
            jax.ShapeDtypeStruct((rows, width), F32),
            jax.ShapeDtypeStruct((8, 128), F32),
        ),
        in_specs=[whole] * 3,
        out_specs=(anywhere, anywhere, whole),
        scratch_shapes=scratch,
        compiler_params=pltpu.CompilerParams(
            collective_id=0, has_side_effects=True, vmem_limit_bytes=60 * 2**20),
        name="swav",
    )(slow_embed, fast_embed, prototypes)
    totals = jnp.sum(sums, axis=1)
    proto_entries = float(protos * n_p * width)
    embed_entries = float(2 * clips * n_b * width)
    proto_factor = lax.rsqrt(totals[0] / proto_entries + NORM_EPS)
    embed_factor = lax.rsqrt(totals[1] / embed_entries + NORM_EPS)
    return (dw * proto_factor, dx[:clips] * embed_factor, dx[clips:] * embed_factor)


def solution(mesh):
    placed = (P("batch", None), P("batch", None), P("proto", None))
    return jax.shard_map(
        body,
        mesh=mesh,
        in_specs=placed,
        out_specs=(P("proto", None), P("batch", None), P("batch", None)),
        check_vma=False,
    )
```

time: 717 us -> 178 us (0.25)
  blocking collectives: 352 us -> 0 us
  waiting for transfers between devices: 213 us -> 0 us
  Pallas kernels: 0 us -> 170 us
  other arithmetic: 108 us -> 5.44 us
  matrix products: 26.5 us -> 0 us
  between operations: 16.9 us -> 2.03 us
    psum x7 -> x0, blocking collectives: 352 us -> none  [the longest x3 155 us: body(): lax.psum(jnp.sum(code_table * clip_scale[:, :, None], axis=1), 'batch')]
    psum x2 -> x0, waiting for transfers between devices: 213 us -> none  [the longest x1 116 us: body(): grad_proto_unit = lax.psum(proto_terms, 'batch')]
    pallas_call x0 -> x1, Pallas kernels: none -> 170 us  [body(): pl.pallas_call(functools.partial(kernel, (clips, protos, width, n_z, n_p)...]
    reduce_sum x9 -> x1, other arithmetic: 50.2 us -> 0.79 us  [body(): totals = jnp.sum(sums, axis=1)]
    dot_general x3 -> x0, matrix products: 26.5 us -> none  [the longest x1 9.21 us: body(): jnp.einsum('vbd,kd->vbk', unit_b, proto_b, preferred_element_type=jnp.flo...]
    sub x1 -> x0, other arithmetic: 19.2 us -> none  [body(): probs[0] - codes[1]]
    div x6 -> x0, other arithmetic: 18.4 us -> none  [the longest x1 18.3 us: body(): probs = soft_exp / denominator[:, :, None]]
    mul x3 -> x2, other arithmetic: 19.9 us -> 4.65 us  [the longest x1 3.2 us: body(): dw * proto_factor]
  transfers between devices with their start and end apart: 2 -> 0, of which waited for: 2 -> 0; matrix products, arithmetic and copies ran while one was open for 2% -> 0% of each run, Pallas kernels for 0% -> 0%
where the time goes in v1:
time: 178 us
  Pallas kernels  170 us (96%)
  other arithmetic  5.44 us (3%)
  between operations  2.03 us (1%)
    pallas_call x1, Pallas kernels, body(): pl.pallas_call(functools.partial(kernel, (clips, protos, width, n_z, n_p)...  170 us

profile of v1, /device:TPU:1, one launch (start us, length us, event | category | flops | bytes accessed | tf_op | source)
XLA Modules:
  0.0 178.0 jit_solution(9677565757283048)
XLA Ops:
  0.6 170.0 %swav.1 = (f32[2048,256]{1,0:T(8,128)}, f32[2048,256]{1,0:T(8,128)}, f32[8,128]{1,0:T(8,128)}) custom-call(bf16[1024,256]{1,0:T(8,128)(2,1)} %slow_ref.1, bf16[1024,256]{1,0:T(8,128)(2,1)} %fast_ref.1, f32[2048,256]{1,0:T(8,128)} %proto_ref.1), custom_call_target="tpu_custom_call" | custom-call | tf_op jit(solution)/shard_map/swav/pallas_call | solution.py:385
  170.6 0.8 reduce_sum.9
  171.4 0.6 fusion
  173.3 0.0 copy-start
  173.4 3.2 %broadcast_multiply_fusion = f32[2048,256]{1,0:T(8,128)} fusion(f32[2048,256]{1,0:T(8,128)} %get-tuple-element.6, f32[]{:T(128)} %bitcast), kind=kLoop, calls=%fused_computation.2 | loop fusion | flops 524288 | bytes 4194308 | tf_op jit(solution)/shard_map/mul | solution.py:404
  176.6 0.0 copy-done
  176.6 1.5 slice_multiply_fusion
Async XLA Ops:
  173.3 3.2 %copy-start = (f32[2048,256]{1,0:T(8,128)S(1)}, f32[2048,256]{1,0:T(8,128)}, u32[]{:S(2)}) copy-start(f32[2048,256]{1,0:T(8,128)} %get-tuple-element.8) | copy-start | bytes 6291460

commit v2 on v1

--- a/solution.py
+++ b/solution.py
@@ -8,6 +8,7 @@
 from jax.sharding import PartitionSpec as P
 
 ITERS = 3
+COPIES = 128
 NORM_EPS = 1e-06
 MESH = pl.DeviceIdType.MESH
 F32 = jnp.float32
@@ -28,13 +29,12 @@
 def kernel(
     dims,
     slow_ref, fast_ref, proto_ref,
-    dw_ref, dx_ref, sum_ref,
+    dw_ref, dx_ref, wf_ref, xf_ref,
     table, grads, unit_b, unit_t, proto_b, partial, clip_b, soft_b, code_b,
-    du, dct, dc_pair, dc_half, du_recv, dc_recv,
-    col_z, col_pair, row_recv, den_recv, sq_p, sq_z, sq_pair, own_dx, own_dw,
+    du, dct, dc_pair, dc_half, rs_buf, rs_small, z_buf, agx, agw,
+    col_z, col_pair, row_recv, den_recv, sq_p, sq_z, sq_pair,
     send_sem, pair_send, col_sem, colp_sem, row_sem, den_sem, den_send,
-    du_sem, dcp_sem, dc_sem, sqp_sem, sqz_sem, sqr_sem, agx_sem, agw_sem, agwp_sem,
-    du_send, dc_send, agx_send, agw_send, agwp_send, local_sem,
+    sqp_sem, sqz_sem, out_sem, in_sem, local_sem,
 ):
     clips, protos, width, n_z, n_p = dims
     batch_me = lax.axis_index("batch")
@@ -234,40 +234,207 @@
 
     lax.fori_loop(0, row_blocks, transpose_unit, 0)
 
-    def dc_dot(i, carry):
-        at = pl.ds(pl.multiple_of(i * 256, 256), 256)
-        out = jnp.dot(unit_t[...], grads[:, at], preferred_element_type=F32)
-        dct[2 * i] = out[:, :128]
-        dct[2 * i + 1] = out[:, 128:]
+    pending = []
+    counter = [0]
+
+    def send(src, dst, device):
+        n = counter[0]
+        counter[0] += 1
+        copy = remote(src, dst, out_sem.at[n], in_sem.at[n], device)
+        copy.start()
+        pending.append(copy)
+        return copy
+
+    def add_to(ref, value):
+        ref[...] = ref[...] + value
+
+    x, y = me_p // 4, me_p % 4
+    x_next = {"proto": (x + 1) % 4 * 4 + y}
+    x_prev = {"proto": (x + 3) % 4 * 4 + y}
+    y_next = {"proto": x * 4 + (y + 1) % 4}
+    y_prev = {"proto": x * 4 + (y + 3) % 4}
+    z_next, z_prev = z_id(1), z_id(n_z - 1)
+
+    class Scatter4:
+        def __init__(self, view, me, ahead, behind, buf):
+            self.view, self.me, self.ahead, self.behind, self.buf = view, me, ahead, behind, buf
+            self.c = {}
+
+        def send(self, slot, dest, part):
+            device = self.ahead if slot < 3 else self.behind
+            self.c[slot] = send(self.view(dest, part), self.buf.at[slot], device)
+
+        def start(self):
+            m = self.me
+            self.send(0, (m + 2) % 4, 0)
+            self.send(3, (m + 2) % 4, 1)
+            self.send(1, (m + 1) % 4, 1)
+            self.send(4, (m + 3) % 4, 0)
+
+        def mid(self):
+            m = self.me
+            self.c[0].wait_recv()
+            add_to(self.view((m + 1) % 4, 0), self.buf[0])
+            self.send(2, (m + 1) % 4, 0)
+            self.c[3].wait_recv()
+            add_to(self.view((m + 3) % 4, 1), self.buf[3])
+            self.send(5, (m + 3) % 4, 1)
+
+        def finish(self):
+            for slot in (1, 4, 2, 5):
+                self.c[slot].wait_recv()
+            add_to(self.view(self.me, 0), self.buf[2] + self.buf[4])
+            add_to(self.view(self.me, 1), self.buf[1] + self.buf[5])
+
+    class Gather4:
+        def __init__(self, view, me, ahead, behind):
+            self.view, self.me, self.ahead, self.behind = view, me, ahead, behind
+            self.c = {}
+
+        def send(self, slot, owner, part):
+            spot = self.view(owner, part)
+            self.c[slot] = send(spot, spot, self.ahead if slot < 3 else self.behind)
+
+        def start(self):
+            self.send(0, self.me, 0)
+            self.send(3, self.me, 1)
+            self.send(1, self.me, 1)
+            self.send(4, self.me, 0)
+
+        def mid(self):
+            self.c[0].wait_recv()
+            self.send(2, (self.me + 3) % 4, 0)
+            self.c[3].wait_recv()
+            self.send(5, (self.me + 1) % 4, 1)
+
+        def finish(self):
+            for slot in (1, 4, 2, 5):
+                self.c[slot].wait_recv()
+
+    def quarter(half, part):
+        return pl.ds(half * 64 + part * 32, 32)
+
+    def along_x(ref, half):
+        return lambda at, part: ref.at[at, :, quarter(half, part), :]
+
+    def along_y(ref, half):
+        return lambda at, part: ref.at[:, at, quarter(half, part), :]
+
+    def in_x(ref, half):
+        return lambda at, part: ref.at[at, y, quarter(half, part), :]
+
+    def in_y(ref, half):
+        return lambda at, part: ref.at[x, at, quarter(half, part), :]
+
+    hops = (4, 3, 3, 2, 2, 1, 1)
+
+    class ScatterZ:
+        def __init__(self):
+            self.c = {}
+
+        def view(self, dest, part):
+            return dc_half.at[dest, pl.ds(part * 128, 128), :]
+
+        def step(self, i):
+            part = i % 2
+            for way in (0, 1):
+                dest = (me_z + (hops[i] if way == 0 else n_z - hops[i])) % n_z
+                spot = self.view(dest, part ^ way)
+                if i >= 2:
+                    self.c[way, i - 2].wait_recv()
+                    add_to(spot, z_buf[way, i - 2])
+                self.c[way, i] = send(spot, z_buf.at[way, i], z_prev if way else z_next)
+
+        def finish(self):
+            for way in (0, 1):
+                for i in (5, 6):
+                    self.c[way, i].wait_recv()
+                    add_to(self.view(me_z, i % 2 ^ way), z_buf[way, i])
+
+    class GatherZ:
+        def __init__(self):
+            self.c = {}
+            self.p = []
+
+        def view(self, owner, part):
+            return agw.at[core * n_z + owner, pl.ds(part * 64, 64), :]
+
+        def came(self, way, i):
+            far = i // 2 + 1
+            owner = (me_z + (far if way else n_z - far)) % n_z
+            return self.view(owner, i % 2 ^ way)
+
+        def relay(self, way, i):
+            self.c[way, i].wait_recv()
+            spot = self.came(way, i)
+            self.p.append(send(spot, spot, partner))
+            return spot
+
+        def step(self, i):
+            for way in (0, 1):
+                if i >= 2:
+                    self.c[way, i - 2].wait_recv()
+                    spot = self.came(way, i - 2)
+                else:
+                    spot = self.view(me_z, i % 2 ^ way)
+                self.c[way, i] = send(spot, spot, z_prev if way else z_next)
+                if i >= 2 or way == 0:
+                    self.p.append(send(spot, spot, partner))
+
+        def finish(self):
+            for way in (0, 1):
+                for i in (5, 6):
+                    self.relay(way, i)
+
+    def dc_dot(first_chunk):
+        def step(i, carry):
+            c = first_chunk + 2 * i
+            at = pl.ds(pl.multiple_of(c * 128, 256), 256)
+            out = jnp.dot(unit_t[...], grads[:, at], preferred_element_type=F32)
+            dct[c] = out[:, :128]
+            dct[c + 1] = out[:, 128:]
+            return carry
+
+        lax.fori_loop(0, n_z // 2, step, 0)
+
+    theirs = (1 - core) * n_z
+    dc_dot(theirs)
+    pair_copy = send(dct.at[pl.ds(theirs, n_z)], dc_pair, partner)
+
+    def du_dot(i, carry):
+        at = pl.ds(pl.multiple_of(i * 512, 512), 512)
+        out = jnp.dot(grads[at, :], proto_b[...], preferred_element_type=F32)
+        du[i] = out.reshape(4, 128, width)
         return carry
 
-    lax.fori_loop(0, protos // 256, dc_dot, 0)
-    half = pl.ds((1 - core) * n_z, n_z)
-    pair_copy = remote(dct.at[half], dc_pair, pair_send, dcp_sem, partner)
-    pair_copy.start()
-
-    def du_dot(i, carry):
-        at = pl.ds(pl.multiple_of(i * 256, 256), 256)
-        out = jnp.dot(grads[at, :], proto_b[...], preferred_element_type=F32)
-        du[2 * i] = out[:128, :]
-        du[2 * i + 1] = out[128:, :]
-        return carry
-
-    lax.fori_loop(0, rows // 256, du_dot, 0)
-    du_copies = []
-    for d in range(1, n_p):
-        copy = remote(du.at[(me_p + d) % n_p], du_recv.at[me_p], du_send.at[d], du_sem.at[d], p_id(d))
-        copy.start()
-        du_copies.append(copy)
-
-    pair_copy.wait()
+    lax.fori_loop(0, rows // 512, du_dot, 0)
+    a1 = Scatter4(along_x(du, 0), x, x_next, x_prev, rs_buf.at[0])
+    b1 = Scatter4(along_y(du, 1), y, y_next, y_prev, rs_buf.at[1])
+    a2 = Scatter4(in_y(du, 0), y, y_next, y_prev, rs_small.at[0])
+    b2 = Scatter4(in_x(du, 1), x, x_next, x_prev, rs_small.at[1])
+    zs, zg = ScatterZ(), GatherZ()
+    a1.start()
+    b1.start()
+
+    dc_dot(core * n_z)
+    pair_copy.wait_recv()
     for i in range(n_z):
         dc_half[i] = dct[core * n_z + i] + dc_pair[i]
-    dc_copies = []
-    for d in range(1, n_z):
-        copy = remote(dc_half.at[(me_z + d) % n_z], dc_recv.at[me_z], dc_send.at[d], dc_sem.at[d], z_id(d))
-        copy.start()
-        dc_copies.append(copy)
+    zs.step(0)
+    zs.step(1)
+    a1.mid()
+    b1.mid()
+    zs.step(2)
+    zs.step(3)
+    zs.step(4)
+    a1.finish()
+    a2.start()
+    b1.finish()
+    b2.start()
+    zs.step(5)
+    zs.step(6)
+    a2.mid()
+    b2.mid()
 
     def project(grad, raw):
         unit, inverse = normalized(raw)
@@ -278,64 +445,70 @@
         sq = block * block
         return jnp.sum(sq[:, :128] + sq[:, 128:], axis=0, keepdims=True)
 
-    du_recv[me_p] = du[me_p]
-    for copy in du_copies:
-        copy.wait()
-    total = total_of(du_recv, n_p)
+    zs.finish()
+    mine = core * n_z + me_z
+    dw_own = project(dc_half[me_z].T, proto_ref[pl.ds(pl.multiple_of(mine * 128, 128), 128), :])
+    agw[mine] = dw_own
+    zg.step(0)
+    zg.step(1)
+    sq_p[me_p, 0:1, :] = lanes_square(dw_own)
+
+    a2.finish()
+    b2.finish()
     at = pl.ds(pl.multiple_of((me_p % view_blocks) * 128, 128), 128)
     is_slow = me_p < view_blocks
     raw = jnp.where(is_slow, slow_ref[at, :].astype(F32), fast_ref[at, :].astype(F32))
-    dx_own = project(total, raw)
-    own_dx[...] = dx_own
-    agx = []
-    spot = dx_ref.at[pl.ds(pl.multiple_of(me_p * 128, 128), 128), :]
-    for d in range(1, n_p):
-        copy = remote(own_dx, spot, agx_send.at[d], agx_sem.at[d], p_id(d))
-        copy.start()
-        agx.append(copy)
-    local_x = pltpu.make_async_copy(own_dx, spot, local_sem.at[0])
-    local_x.start()
-
-    dc_recv[me_z] = dc_half[me_z]
-    for copy in dc_copies:
-        copy.wait()
-    total = total_of(dc_recv, n_z).T
-    at = pl.ds(pl.multiple_of((core * n_z + me_z) * 128, 128), 128)
-    dw_own = project(total, proto_ref[at, :])
-    own_dw[...] = dw_own
-    agw = []
-    spot_w = dw_ref.at[at, :]
-    for d in range(1, n_z):
-        copy = remote(own_dw, spot_w, agw_send.at[d], agw_sem.at[d], z_id(d))
-        copy.start()
-        agw.append(copy)
-    local_w = pltpu.make_async_copy(own_dw, spot_w, local_sem.at[1])
-    local_w.start()
-
-    sq_p[me_p, 0:1, :] = lanes_square(dw_own)
+    dx_own = project(du[x, y], raw)
+    agx[x, y] = dx_own
+    ga1 = Gather4(in_y(agx, 0), y, y_next, y_prev)
+    gb1 = Gather4(in_x(agx, 1), x, x_next, x_prev)
+    ga2 = Gather4(along_x(agx, 0), x, x_next, x_prev)
+    gb2 = Gather4(along_y(agx, 1), y, y_next, y_prev)
+    ga1.start()
+    gb1.start()
     sq_p[me_p, 1:2, :] = lanes_square(dx_own)
     sq_p[me_p, 2:8, :] = jnp.zeros((6, 128), F32)
-    for copy in start_all(sq_p, me_p, n_p, p_id, send_sem, sqp_sem):
+    sq_copies = start_all(sq_p, me_p, n_p, p_id, send_sem, sqp_sem)
+    zg.step(2)
+    zg.step(3)
+    ga1.mid()
+    gb1.mid()
+    zg.step(4)
+    ga1.finish()
+    ga2.start()
+    gb1.finish()
+    gb2.start()
+    for copy in sq_copies:
         copy.wait()
     sq_z[me_z] = total_of(sq_p, n_p)
-    for copy in start_all(sq_z, me_z, n_z, z_id, send_sem, sqz_sem):
+    sq_copies = start_all(sq_z, me_z, n_z, z_id, send_sem, sqz_sem)
+    zg.step(5)
+    zg.step(6)
+    ga2.mid()
+    gb2.mid()
+    for copy in sq_copies:
         copy.wait()
     sq_pair[core] = total_of(sq_z, n_z)
-    copy = remote(sq_pair.at[core], sq_pair.at[core], pair_send, sqr_sem, partner)
-    copy.start()
-    copy.wait()
-    sum_ref[...] = sq_pair[0] + sq_pair[1]
-
-    for copy in agw:
-        copy.wait()
+    pair_copy = send(sq_pair.at[core], sq_pair.at[core], partner)
+    zg.finish()
+    for copy in zg.p:
+        copy.wait_recv()
+    local_w = pltpu.make_async_copy(agw, dw_ref, local_sem.at[0])
+    local_w.start()
+    pair_copy.wait_recv()
+    square = jnp.sum(sq_pair[0] + sq_pair[1], axis=1, keepdims=True)
+    entries = float(protos_all * width), float(2 * clips_all * width)
+    for i, out in enumerate((wf_ref, xf_ref)):
+        out[...] = jnp.broadcast_to(
+            lax.rsqrt(square[i:i + 1, :] / entries[i] + NORM_EPS), (8, width))
+    ga2.finish()
+    gb2.finish()
+    local_x = pltpu.make_async_copy(agx, dx_ref, local_sem.at[1])
+    local_x.start()
+    for copy in pending:
+        copy.wait_send()
     local_w.wait()
-    half_rows = pl.ds(pl.multiple_of(core * n_z * 128, 128), n_z * 128)
-    copy = remote(dw_ref.at[half_rows, :], dw_ref.at[half_rows, :], agwp_send, agwp_sem, partner)
-    copy.start()
-    copy.wait()
     local_x.wait()
-    for copy in agx:
-        copy.wait()
 
 
 def body(slow_embed, fast_embed, prototypes):
@@ -359,12 +532,15 @@
         vmem((rows, 128), F32),
         vmem((rows, 128), F32),
         vmem((rows, 128), F32),
-        vmem((n_p, rows // n_p, width), F32),
+        vmem((4, 4, 128, width), F32),
         vmem((lane_chunks, width, 128), F32),
         vmem((n_z, width, 128), F32),
         vmem((n_z, width, 128), F32),
-        vmem((n_p, rows // n_p, width), F32),
-        vmem((n_z, width, 128), F32),
+        vmem((2, 6, 4, 32, width), F32),
+        vmem((2, 6, 32, width), F32),
+        vmem((2, 7, 128, 128), F32),
+        vmem((4, 4, 128, width), F32),
+        vmem((lane_chunks, 128, width), F32),
         vmem((ITERS, n_z, 2 * lane_chunks, 128), F32),
         vmem((ITERS, 2, 2 * lane_chunks, 128), F32),
         vmem((ITERS, n_p, row_blocks, 128), F32),
@@ -372,36 +548,33 @@
         vmem((n_p, 8, 128), F32),
         vmem((n_z, 8, 128), F32),
         vmem((2, 8, 128), F32),
-        vmem((rows // n_p, width), F32),
-        vmem((128, width), F32),
         DMA((16,)), DMA(()), DMA((ITERS, n_z)), DMA((ITERS,)), DMA((ITERS, n_p)),
         DMA((n_p,)), DMA((n_p,)),
-        DMA((n_p,)), DMA(()), DMA((n_z,)), DMA((n_p,)), DMA((n_z,)), DMA(()),
-        DMA((n_p,)), DMA((n_z,)), DMA(()),
-        DMA((n_p,)), DMA((n_z,)), DMA((n_p,)), DMA((n_z,)), DMA(()), DMA((2,)),
+        DMA((n_p,)), DMA((n_z,)), DMA((COPIES,)), DMA((COPIES,)), DMA((2,)),
     ]
     whole = pl.BlockSpec(memory_space=pltpu.VMEM)
     anywhere = pl.BlockSpec(memory_space=pl.ANY)
-    dw, dx, sums = pl.pallas_call(
+    dw, dx, dw_factor, dx_factor = pl.pallas_call(
         functools.partial(kernel, (clips, protos, width, n_z, n_p)),
         out_shape=(
-            jax.ShapeDtypeStruct((protos, width), F32),
-            jax.ShapeDtypeStruct((rows, width), F32),
-            jax.ShapeDtypeStruct((8, 128), F32),
+            jax.ShapeDtypeStruct((lane_chunks, 128, width), F32),
+            jax.ShapeDtypeStruct((4, 4, 128, width), F32),
+            jax.ShapeDtypeStruct((8, width), F32),
+            jax.ShapeDtypeStruct((8, width), F32),
         ),
         in_specs=[whole] * 3,
-        out_specs=(anywhere, anywhere, whole),
+        out_specs=(anywhere, anywhere, whole, whole),
         scratch_shapes=scratch,
         compiler_params=pltpu.CompilerParams(
             collective_id=0, has_side_effects=True, vmem_limit_bytes=60 * 2**20),
         name="swav",
     )(slow_embed, fast_embed, prototypes)
-    totals = jnp.sum(sums, axis=1)
-    proto_entries = float(protos * n_p * width)
-    embed_entries = float(2 * clips * n_b * width)
-    proto_factor = lax.rsqrt(totals[0] / proto_entries + NORM_EPS)
-    embed_factor = lax.rsqrt(totals[1] / embed_entries + NORM_EPS)
-    return (dw * proto_factor, dx[:clips] * embed_factor, dx[clips:] * embed_factor)
+    dw = (dw.reshape(protos // 8, 8, width) * dw_factor).reshape(protos, width)
+    dx = dx.reshape(rows // 8, 8, width)
+    half = clips // 8
+    slow = (dx[:half] * dx_factor).reshape(clips, width)
+    fast = (dx[half:] * dx_factor).reshape(clips, width)
+    return (dw, slow, fast)
 
 
 def solution(mesh):

time: 178 us -> 129 us (0.72)
  Pallas kernels: 170 us -> 123 us
    pallas_call x1, Pallas kernels: 170 us -> 123 us  [body(): pl.pallas_call(functools.partial(kernel, (clips, protos, width, n_z, n_p)...]
where the time goes in v2:
time: 129 us
  Pallas kernels  123 us (95%)
  other arithmetic  4.66 us (4%)
    pallas_call x1, Pallas kernels, body(): pl.pallas_call(functools.partial(kernel, (clips, protos, width, n_z, n_p)...  123 us
    mul x1, other arithmetic, body(): dw = (dw.reshape(protos // 8, 8, width) * dw_factor).reshape(protos, width)  3.2 us

profile of v2, /device:TPU:1, one launch (start us, length us, event | category | flops | bytes accessed | tf_op | source)
XLA Modules:
  0.0 128.7 jit_solution(14643097241516378810)
XLA Ops:
  0.6 122.7 %swav.1 = (f32[16,128,256]{2,1,0:T(8,128)}, f32[4,4,128,256]{3,2,1,0:T(8,128)}, f32[8,256]{1,0:T(8,128)}, f32[8,256]{1,0:T(8,128)}) custom-call(bf16[1024,256]{1,0:T(8,128)(2,1)} %slow_ref.1, bf16[1024,256]{1,0:T(8,128)(2,1)} %fast_ref.1, f32[2048,256]{1,0:T(8,128)} %proto_ref.1), custom_call_target="tpu_custom_call" | custom-call | tf_op jit(solution)/shard_map/swav/pallas_call | solution.py:557
  123.3 0.0 copy-start
  123.3 3.2 %bitcast_multiply_fusion = f32[2048,256]{1,0:T(8,128)} fusion(f32[16,128,256]{2,1,0:T(8,128)} %get-tuple-element.7, f32[8,256]{1,0:T(8,128)} %get-tuple-element.8), kind=kLoop, calls=%fused_computation | loop fusion | flops 524288 | bytes 4202496 | tf_op jit(solution)/shard_map/mul | solution.py:572
  126.5 0.0 copy-done
  126.5 0.0 copy-start.1
  126.5 0.2 fusion
  126.7 0.5 copy-done.1
  127.2 1.5 %bitcast_multiply_fusion.1 = (f32[1024,256]{1,0:T(8,128)}, f32[1024,256]{1,0:T(8,128)}) fusion(f32[2,4,128,256]{3,2,1,0:T(8,128)S(1)} %get-tuple-element.11, f32[8,256]{1,0:T(8,128)S(1)} %copy-done.1, f32[2,4,128,256]{3,2,1,0:T(8,128)S(1)} %get-tuple-element.12), kind=kLoop, calls=%fused_computation.1 | loop fusion | flops 524288 | bytes 4202496 | tf_op jit(solution)/shard_map/mul | solution.py:576
Async XLA Ops:
  123.3 3.2 %copy-start = (f32[4,4,128,256]{3,2,1,0:T(8,128)S(1)}, f32[4,4,128,256]{3,2,1,0:T(8,128)}, u32[]{:S(2)}) copy-start(f32[4,4,128,256]{3,2,1,0:T(8,128)} %get-tuple-element.9) | copy-start | bytes 6291460
  126.5 0.7 copy-start.1

commit v3 on v2

--- a/solution.py
+++ b/solution.py
@@ -30,10 +30,10 @@
     dims,
     slow_ref, fast_ref, proto_ref,
     dw_ref, dx_ref, wf_ref, xf_ref,
-    table, grads, unit_b, unit_t, proto_b, partial, clip_b, soft_b, code_b,
+    table, grads, unit_b, unit_t, proto_b, scale, clip_b, soft_b, code_b,
     du, dct, dc_pair, dc_half, rs_buf, rs_small, z_buf, agx, agw,
     col_z, col_pair, row_recv, den_recv, sq_p, sq_z, sq_pair,
-    send_sem, pair_send, col_sem, colp_sem, row_sem, den_sem, den_send,
+    send_sem, col_send, col_sem, colp_send, colp_sem, row_send, row_sem, den_sem, den_send,
     sqp_sem, sqz_sem, out_sem, in_sem, local_sem,
 ):
     clips, protos, width, n_z, n_p = dims
@@ -81,52 +81,11 @@
     def chunk(c):
         return slice(c * 128, (c + 1) * 128)
 
-    step_w = 512
-    for v in range(2):
-        def first(i, cols):
-            at = pl.ds(pl.multiple_of(i * 128, 128), 128)
-            glob = pl.ds(pl.multiple_of(v * clips + i * 128, 128), 128)
-            unit, _ = normalized(embeds[v][at, :].astype(F32))
-            ub = unit.astype(BF16)
-            unit_b[glob, :] = ub
-            den = jnp.zeros((128, 128), F32)
-            cols = list(cols)
-            for k in range(protos // step_w):
-                score = lax.dot_general(
-                    ub, proto_b[k * step_w:(k + 1) * step_w, :],
-                    (((1,), (1,)), ((), ())), preferred_element_type=F32)
-                soft = jnp.exp(score * 10.0)
-                table[glob, k * step_w:(k + 1) * step_w] = soft
-                for j in range(step_w // 128):
-                    t = soft[:, chunk(j)]
-                    den = den + t
-                    c = k * (step_w // 128) + j
-                    cols[c] = cols[c] + fold8(t * t)
-            partial[glob, :] = den
-            return tuple(cols)
-
-        cols = lax.fori_loop(
-            0, view_blocks, first,
-            tuple(jnp.zeros((8, 128), F32) for _ in range(lane_chunks)))
-        for c in range(lane_chunks):
-            col_z[0, me_z, v * lane_chunks + c:v * lane_chunks + c + 1, :] = jnp.sum(
-                cols[c], axis=0, keepdims=True)
-
-    pl.semaphore_wait(barrier, n_p - 1 + n_z - 1 + 1)
-
-    ones = jnp.ones((8, 128), F32)
-
-    def dense_rows(store):
-        for v in range(2):
-            total = lax.dot_general(
-                ones, partial[v * clips:(v + 1) * clips, :], (((1,), (1,)), ((), ())),
-                precision=lax.Precision.HIGHEST, preferred_element_type=F32)
-            for i in range(view_blocks):
-                store(v * view_blocks + i, total[0:1, chunk(i)])
-
-    def spread(values, target):
-        for i in range(row_blocks):
-            target[chunk(i), :] = jnp.broadcast_to(values[i:i + 1, :], (128, 128)).T
+    def total_of(ref, count):
+        acc = ref[0]
+        for i in range(1, count):
+            acc = acc + ref[i]
+        return acc
 
     def start_all(ref, me, count, ids, send, recv):
         copies = []
@@ -136,103 +95,147 @@
             copies.append(copy)
         return copies
 
-    def total_of(ref, count):
-        acc = ref[0]
-        for i in range(1, count):
-            acc = acc + ref[i]
-        return acc
-
-    def col_total(it):
-        buf = col_z.at[it]
-        for copy in start_all(buf, me_z, n_z, z_id, send_sem, col_sem.at[it]):
-            copy.wait()
-        pair = col_pair.at[it]
-        pair[core] = total_of(buf, n_z)
-        copy = remote(pair.at[core], pair.at[core], pair_send, colp_sem.at[it], partner)
+    zero = jnp.zeros((8, 128), F32)
+
+    def put_cols(it, v, cols):
+        for c in range(lane_chunks):
+            col_z[it, v, me_z, c:c + 1, :] = jnp.sum(cols[c], axis=0, keepdims=True)
+        return start_all(col_z.at[it, v], me_z, n_z, z_id, col_send.at[it, v], col_sem.at[it, v])
+
+    def lane_sums(block):
+        return jnp.sum(block.T, axis=0, keepdims=True)
+
+    def spread(values, v, target):
+        for i in range(view_blocks):
+            at = slice(v * clips + i * 128, v * clips + (i + 1) * 128)
+            target[at, :] = jnp.broadcast_to(values[i:i + 1, :], (128, 128)).T
+
+    step_m, step_w = 256, 512
+
+    def first_pass(v):
+        def step(i, cols):
+            at = pl.ds(pl.multiple_of(i * step_m, step_m), step_m)
+            glob = pl.ds(pl.multiple_of(v * clips + i * step_m, step_m), step_m)
+            unit, _ = normalized(embeds[v][at, :].astype(F32))
+            ub = unit.astype(BF16)
+            unit_b[glob, :] = ub
+            den = jnp.zeros((step_m, 128), F32)
+            cols = list(cols)
+            for k in range(protos // step_w):
+                score = lax.dot_general(
+                    ub, proto_b[k * step_w:(k + 1) * step_w, :],
+                    (((1,), (1,)), ((), ())), preferred_element_type=F32)
+                soft = jnp.exp(score * 10.0)
+                code = soft * soft
+                table[glob, k * step_w:(k + 1) * step_w] = code
+                for j in range(step_w // 128):
+                    den = den + soft[:, chunk(j)]
+                    c = k * (step_w // 128) + j
+                    cols[c] = cols[c] + fold8(code[:, chunk(j)])
+            for j in range(step_m // 128):
+                den_recv[me_p, pl.ds(v * view_blocks + i * (step_m // 128) + j, 1), :] = lane_sums(den[chunk(j), :])
+            return tuple(cols)
+
+        return lax.fori_loop(0, clips // step_m, step, (zero,) * lane_chunks)
+
+    def cols_pass(v):
+        def step(i, cols):
+            at = pl.ds(pl.multiple_of(v * clips + i * 64, 64), 64)
+            s = clip_b[at, :]
+            return tuple(cols[c] + fold8(table[at, chunk(c)] * s) for c in range(lane_chunks))
+
+        return lax.fori_loop(0, clips // 64, step, (zero,) * lane_chunks)
+
+    def rows_pass(it, v):
+        def step(i, carry):
+            for j in range(2):
+                block = 2 * i + j
+                at = pl.ds(pl.multiple_of(v * clips + block * 128, 128), 128)
+                acc = jnp.zeros((128, 128), F32)
+                for c in range(lane_chunks):
+                    acc = acc + table[at, chunk(c)] * scale[v, c:c + 1, :]
+                row_recv[it, v, me_p, pl.ds(block, 1), :] = lane_sums(acc)
+            return carry
+
+        lax.fori_loop(0, view_blocks // 2, step, 0)
+        return start_all(row_recv.at[it, v], me_p, n_p, p_id, row_send.at[it, v], row_sem.at[it, v])
+
+    def wait_all(copies):
+        for copy in copies:
+            copy.wait_recv()
+        sends.extend(copies)
+
+    def pair_start(it, v, copies):
+        wait_all(copies)
+        pair = col_pair.at[it, v]
+        pair[core] = total_of(col_z.at[it, v], n_z)
+        copy = remote(pair.at[core], pair.at[core], colp_send.at[it, v], colp_sem.at[it, v], partner)
         copy.start()
-        copy.wait()
-        return pair[0] + pair[1]
-
-    def row_total(it):
-        buf = row_recv.at[it]
-
-        def put(i, value):
-            buf[me_p, i:i + 1, :] = value
-
-        dense_rows(put)
-        for copy in start_all(buf, me_p, n_p, p_id, send_sem, row_sem.at[it]):
-            copy.wait()
-        return total_of(buf, n_p)
-
-    def put_den(i, value):
-        den_recv[me_p, i:i + 1, :] = value
-
-    dense_rows(put_den)
+        return copy
+
+    sends = []
+    z_copies = [None, None]
+    row_copies = [None, None]
+    z_cols = first_pass(0)
+    pl.semaphore_wait(barrier, n_p - 1 + n_z - 1 + 1)
+    z_copies[0] = put_cols(0, 0, z_cols)
+    z_copies[1] = put_cols(0, 1, first_pass(1))
     den_copies = start_all(den_recv, me_p, n_p, p_id, den_send, den_sem)
 
-    scale = None
-    for it in range(ITERS):
-        if it > 0:
-            for v in range(2):
-                def cols_pass(i, cols):
-                    at = pl.ds(pl.multiple_of(v * clips + i * 64, 64), 64)
-                    s = clip_b[at, :]
-                    out = []
-                    for c in range(lane_chunks):
-                        t = table[at, chunk(c)]
-                        out.append(cols[c] + fold8(t * t * s))
-                    return tuple(out)
-
-                cols = lax.fori_loop(
-                    0, clips // 64, cols_pass,
-                    tuple(jnp.zeros((8, 128), F32) for _ in range(lane_chunks)))
-                for c in range(lane_chunks):
-                    col_z[it, me_z, v * lane_chunks + c:v * lane_chunks + c + 1, :] = jnp.sum(
-                        cols[c], axis=0, keepdims=True)
-        scale = 1.0 / (protos_all * col_total(it))
-        for v in range(2):
-            def rows_pass(i, carry):
-                at = pl.ds(pl.multiple_of(v * clips + i * 64, 64), 64)
-                acc = jnp.zeros((64, 128), F32)
-                for c in range(lane_chunks):
-                    t = table[at, chunk(c)]
-                    r = scale[v * lane_chunks + c:v * lane_chunks + c + 1, :]
-                    acc = acc + t * t * r
-                partial[at, :] = acc
-                return carry
-
-            lax.fori_loop(0, clips // 64, rows_pass, 0)
-        row_sum = row_total(it)
-        if it < ITERS - 1:
-            spread(1.0 / (clips_all * row_sum), clip_b)
-    for copy in den_copies:
-        copy.wait()
-    spread(10.0 / total_of(den_recv, n_p), soft_b)
-    spread(10.0 / row_sum, code_b)
-
-    for v in range(2):
+    def transpose_unit(i, carry):
+        at = pl.ds(pl.multiple_of(i * 128, 128), 128)
+        unit_t[:, at] = unit_b[at, :].astype(F32).T.astype(BF16)
+        return carry
+
+    lax.fori_loop(0, row_blocks, transpose_unit, 0)
+
+    def grad_pass(v):
         w = 1 - v
 
-        def grad_pass(i, carry):
+        def step(i, carry):
             mine = pl.ds(pl.multiple_of(v * clips + i * 64, 64), 64)
             other = pl.ds(pl.multiple_of(w * clips + i * 64, 64), 64)
             soft_scale = soft_b[mine, :]
             code_scale = code_b[other, :]
             for c in range(lane_chunks):
-                r = scale[w * lane_chunks + c:w * lane_chunks + c + 1, :]
-                t = table[other, chunk(c)]
-                g = table[mine, chunk(c)] * soft_scale - t * t * r * code_scale
-                grads[mine, chunk(c)] = g.astype(BF16)
+                e = table[mine, chunk(c)]
+                code = table[other, chunk(c)] * scale[w, c:c + 1, :] * code_scale
+                grads[mine, chunk(c)] = (e * lax.rsqrt(e) * soft_scale - code).astype(BF16)
             return carry
 
-        lax.fori_loop(0, clips // 64, grad_pass, 0)
-
-    def transpose_unit(i, carry):
-        at = pl.ds(pl.multiple_of(i * 128, 128), 128)
-        unit_t[:, at] = unit_b[at, :].astype(F32).T.astype(BF16)
-        return carry
-
-    lax.fori_loop(0, row_blocks, transpose_unit, 0)
+        lax.fori_loop(0, clips // 64, step, 0)
+
+    def du_dot(first_step):
+        def step(i, carry):
+            at = pl.ds(pl.multiple_of(i * 512, 512), 512)
+            out = jnp.dot(grads[at, :], proto_b[...], preferred_element_type=F32)
+            du[i] = out.reshape(4, 128, width)
+            return carry
+
+        lax.fori_loop(first_step, first_step + 2, step, 0)
+
+    for it in range(ITERS):
+        pairs = [pair_start(it, v, z_copies[v]) for v in range(2)]
+        for v in range(2):
+            wait_all([pairs[v]])
+            scale[v] = 1.0 / (protos_all * (col_pair[it, v, 0] + col_pair[it, v, 1]))
+            row_copies[v] = rows_pass(it, v)
+        if it == 0:
+            wait_all(den_copies)
+            soft = 10.0 / total_of(den_recv, n_p)
+            for v in range(2):
+                spread(soft[v * view_blocks:(v + 1) * view_blocks], v, soft_b)
+        for v in range(2):
+            wait_all(row_copies[v])
+            row_sum = total_of(row_recv.at[it, v], n_p)
+            if it < ITERS - 1:
+                spread(1.0 / (clips_all * row_sum), v, clip_b)
+                z_copies[v] = put_cols(it + 1, v, cols_pass(v))
+            else:
+                spread(10.0 / row_sum, v, code_b)
+                grad_pass(1 - v)
+                if v == 0:
+                    du_dot(2)
 
     pending = []
     counter = [0]
@@ -401,13 +404,7 @@
     dc_dot(theirs)
     pair_copy = send(dct.at[pl.ds(theirs, n_z)], dc_pair, partner)
 
-    def du_dot(i, carry):
-        at = pl.ds(pl.multiple_of(i * 512, 512), 512)
-        out = jnp.dot(grads[at, :], proto_b[...], preferred_element_type=F32)
-        du[i] = out.reshape(4, 128, width)
-        return carry
-
-    lax.fori_loop(0, rows // 512, du_dot, 0)
+    du_dot(0)
     a1 = Scatter4(along_x(du, 0), x, x_next, x_prev, rs_buf.at[0])
     b1 = Scatter4(along_y(du, 1), y, y_next, y_prev, rs_buf.at[1])
     a2 = Scatter4(in_y(du, 0), y, y_next, y_prev, rs_small.at[0])
@@ -505,7 +502,7 @@
     gb2.finish()
     local_x = pltpu.make_async_copy(agx, dx_ref, local_sem.at[1])
     local_x.start()
-    for copy in pending:
+    for copy in pending + sends:
         copy.wait_send()
     local_w.wait()
     local_x.wait()
@@ -528,7 +525,7 @@
         vmem((rows, width), BF16),
         vmem((width, rows), BF16),
         vmem((protos, width), BF16),
-        vmem((rows, 128), F32),
+        vmem((2, lane_chunks, 128), F32),
         vmem((rows, 128), F32),
         vmem((rows, 128), F32),
         vmem((rows, 128), F32),
@@ -541,14 +538,15 @@
         vmem((2, 7, 128, 128), F32),
         vmem((4, 4, 128, width), F32),
         vmem((lane_chunks, 128, width), F32),
-        vmem((ITERS, n_z, 2 * lane_chunks, 128), F32),
-        vmem((ITERS, 2, 2 * lane_chunks, 128), F32),
-        vmem((ITERS, n_p, row_blocks, 128), F32),
+        vmem((ITERS, 2, n_z, lane_chunks, 128), F32),
+        vmem((ITERS, 2, 2, lane_chunks, 128), F32),
+        vmem((ITERS, 2, n_p, row_blocks // 2, 128), F32),
         vmem((n_p, row_blocks, 128), F32),
         vmem((n_p, 8, 128), F32),
         vmem((n_z, 8, 128), F32),
         vmem((2, 8, 128), F32),
-        DMA((16,)), DMA(()), DMA((ITERS, n_z)), DMA((ITERS,)), DMA((ITERS, n_p)),
+        DMA((16,)), DMA((ITERS, 2, n_z)), DMA((ITERS, 2, n_z)), DMA((ITERS, 2)), DMA((ITERS, 2)),
+        DMA((ITERS, 2, n_p)), DMA((ITERS, 2, n_p)),
         DMA((n_p,)), DMA((n_p,)),
         DMA((n_p,)), DMA((n_z,)), DMA((COPIES,)), DMA((COPIES,)), DMA((2,)),
     ]

time: 129 us -> 113 us (0.88)
  Pallas kernels: 123 us -> 107 us
    pallas_call x1, Pallas kernels: 123 us -> 107 us  [body(): pl.pallas_call(functools.partial(kernel, (clips, protos, width, n_z, n_p)...]
where the time goes in v3:
time: 113 us
  Pallas kernels  107 us (95%)
  other arithmetic  4.66 us (4%)
    pallas_call x1, Pallas kernels, body(): pl.pallas_call(functools.partial(kernel, (clips, protos, width, n_z, n_p)...  107 us
    mul x1, other arithmetic, body(): dw = (dw.reshape(protos // 8, 8, width) * dw_factor).reshape(protos, width)  3.2 us

profile of v3, /device:TPU:1, one launch (start us, length us, event | category | flops | bytes accessed | tf_op | source)
XLA Modules:
  0.0 112.8 jit_solution(4580008495941733260)
XLA Ops:
  0.6 106.8 %swav.1 = (f32[16,128,256]{2,1,0:T(8,128)}, f32[4,4,128,256]{3,2,1,0:T(8,128)}, f32[8,256]{1,0:T(8,128)}, f32[8,256]{1,0:T(8,128)}) custom-call(bf16[1024,256]{1,0:T(8,128)(2,1)} %slow_ref.1, bf16[1024,256]{1,0:T(8,128)(2,1)} %fast_ref.1, f32[2048,256]{1,0:T(8,128)} %proto_ref.1), custom_call_target="tpu_custom_call" | custom-call | tf_op jit(solution)/shard_map/swav/pallas_call | solution.py:555
  107.4 0.0 copy-start
  107.4 3.2 %bitcast_multiply_fusion = f32[2048,256]{1,0:T(8,128)} fusion(f32[16,128,256]{2,1,0:T(8,128)} %get-tuple-element.7, f32[8,256]{1,0:T(8,128)} %get-tuple-element.8), kind=kLoop, calls=%fused_computation | loop fusion | flops 524288 | bytes 4202496 | tf_op jit(solution)/shard_map/mul | solution.py:570
  110.6 0.0 copy-done
  110.6 0.0 copy-start.1
  110.6 0.2 fusion
  110.8 0.5 copy-done.1
  111.3 1.5 %bitcast_multiply_fusion.1 = (f32[1024,256]{1,0:T(8,128)}, f32[1024,256]{1,0:T(8,128)}) fusion(f32[2,4,128,256]{3,2,1,0:T(8,128)S(1)} %get-tuple-element.11, f32[8,256]{1,0:T(8,128)S(1)} %copy-done.1, f32[2,4,128,256]{3,2,1,0:T(8,128)S(1)} %get-tuple-element.12), kind=kLoop, calls=%fused_computation.1 | loop fusion | flops 524288 | bytes 4202496 | tf_op jit(solution)/shard_map/mul | solution.py:574
Async XLA Ops:
  107.4 3.2 %copy-start = (f32[4,4,128,256]{3,2,1,0:T(8,128)S(1)}, f32[4,4,128,256]{3,2,1,0:T(8,128)}, u32[]{:S(2)}) copy-start(f32[4,4,128,256]{3,2,1,0:T(8,128)} %get-tuple-element.9) | copy-start | bytes 6291460
  110.6 0.7 copy-start.1

commit v4 on v3

v4 whole, which is shorter than its diff:
```python
import functools

import jax
import jax.numpy as jnp
from jax import lax
from jax.experimental import pallas as pl
from jax.experimental.pallas import tpu as pltpu
from jax.sharding import PartitionSpec as P

ITERS = 3
COPIES = 192
NORM_EPS = 1e-06
MESH = pl.DeviceIdType.MESH
F32 = jnp.float32
BF16 = jnp.bfloat16


def normalized(rows):
    total = jnp.sum(rows * rows, axis=-1, keepdims=True) + 1e-12
    inverse = 1.0 / jnp.sqrt(total)
    return rows * inverse, inverse


def fold8(block):
    rows, lanes = block.shape
    return jnp.sum(block.reshape(rows // 8, 8, lanes), axis=0)


def kernel(
    dims,
    slow_ref, fast_ref, proto_ref,
    agw, slow_out, fast_out, wf_ref, xf_ref,
    table, grads, unit_b, unit_t, proto_b, scale, clip_b, soft_b, code_b,
    du, dct, dc_pair, dc_half, rs_buf, rs_small, z_buf,
    col_z, col_pair, row_recv, den_recv, sq_p, sq_z,
    send_sem, col_send, col_sem, colp_send, colp_sem, row_send, row_sem, den_sem, den_send,
    sqp_sem, sqz_sem, sqz_send, pair_out, pair_in, out_sem, in_sem,
):
    clips, protos, width, n_z, n_p = dims
    batch_me = lax.axis_index("batch")
    me_p = lax.axis_index("proto")
    me_z = batch_me // 2
    core = batch_me % 2
    clips_all = clips * 2 * n_z
    protos_all = protos * n_p
    rows = 2 * clips
    lane_chunks = protos // 128
    row_blocks = rows // 128
    view_blocks = clips // 128
    embeds = (slow_ref, fast_ref)

    def p_id(d):
        return {"proto": (me_p + d) % n_p}

    def z_id(d):
        return {"batch": ((me_z + d) % n_z) * 2 + core}

    def b_id(d):
        return {"batch": (batch_me + d) % (2 * n_z)}

    partner = {"batch": me_z * 2 + 1 - core}

    def remote(src, dst, send, recv, device):
        return pltpu.make_async_remote_copy(
            src_ref=src, dst_ref=dst, send_sem=send, recv_sem=recv,
            device_id=device, device_id_type=MESH,
        )

    barrier = pltpu.get_barrier_semaphore()
    for d in range(1, n_p):
        pl.semaphore_signal(barrier, inc=1, device_id=p_id(d), device_id_type=MESH)
    for d in range(1, 2 * n_z):
        pl.semaphore_signal(barrier, inc=1, device_id=b_id(d), device_id_type=MESH)

    def proto_norm(i, carry):
        at = pl.ds(pl.multiple_of(i * 128, 128), 128)
        unit, _ = normalized(proto_ref[at, :])
        proto_b[at, :] = unit.astype(BF16)
        return carry

    lax.fori_loop(0, protos // 128, proto_norm, 0)

    def chunk(c):
        return slice(c * 128, (c + 1) * 128)

    def total_of(ref, count):
        acc = ref[0]
        for i in range(1, count):
            acc = acc + ref[i]
        return acc

    def start_all(ref, me, count, ids, send, recv):
        copies = []
        for d in range(1, count):
            copy = remote(ref.at[me], ref.at[me], send.at[d], recv.at[d], ids(d))
            copy.start()
            copies.append(copy)
        return copies

    zero = jnp.zeros((8, 128), F32)

    def put_cols(it, v, cols):
        for c in range(lane_chunks):
            col_z[it, v, me_z, c:c + 1, :] = jnp.sum(cols[c], axis=0, keepdims=True)
        return start_all(col_z.at[it, v], me_z, n_z, z_id, col_send.at[it, v], col_sem.at[it, v])

    def lane_sums(block):
        return jnp.sum(block.T, axis=0, keepdims=True)

    def spread(values, v, target):
        for i in range(view_blocks):
            at = slice(v * clips + i * 128, v * clips + (i + 1) * 128)
            target[at, :] = jnp.broadcast_to(values[i:i + 1, :], (128, 128)).T

    pending = []
    counter = [0]

    def send(src, dst, device):
        n = counter[0]
        counter[0] += 1
        copy = remote(src, dst, out_sem.at[n], in_sem.at[n], device)
        copy.start()
        pending.append(copy)
        return copy

    def add_to(ref, value):
        ref[...] = ref[...] + value

    x, y = me_p // 4, me_p % 4
    x_next = {"proto": (x + 1) % 4 * 4 + y}
    x_prev = {"proto": (x + 3) % 4 * 4 + y}
    y_next = {"proto": x * 4 + (y + 1) % 4}
    y_prev = {"proto": x * 4 + (y + 3) % 4}
    z_next, z_prev = z_id(1), z_id(n_z - 1)

    class Scatter4:
        def __init__(self, view, me, ahead, behind, buf):
            self.view, self.me, self.ahead, self.behind, self.buf = view, me, ahead, behind, buf
            self.c = {}

        def send(self, slot, dest, part):
            device = self.ahead if slot < 3 else self.behind
            self.c[slot] = send(self.view(dest, part), self.buf.at[slot], device)

        def start(self):
            m = self.me
            self.send(0, (m + 2) % 4, 0)
            self.send(3, (m + 2) % 4, 1)
            self.send(1, (m + 1) % 4, 1)
            self.send(4, (m + 3) % 4, 0)

        def mid(self):
            m = self.me
            self.c[0].wait_recv()
            add_to(self.view((m + 1) % 4, 0), self.buf[0])
            self.send(2, (m + 1) % 4, 0)
            self.c[3].wait_recv()
            add_to(self.view((m + 3) % 4, 1), self.buf[3])
            self.send(5, (m + 3) % 4, 1)

        def finish(self):
            for slot in (1, 4, 2, 5):
                self.c[slot].wait_recv()
            add_to(self.view(self.me, 0), self.buf[2] + self.buf[4])
            add_to(self.view(self.me, 1), self.buf[1] + self.buf[5])

    class Gather4:
        def __init__(self, view, me, ahead, behind):
            self.view, self.me, self.ahead, self.behind = view, me, ahead, behind
            self.c = {}

        def send(self, slot, owner, part):
            spot = self.view(owner, part)
            self.c[slot] = send(spot, spot, self.ahead if slot < 3 else self.behind)

        def start(self):
            self.send(0, self.me, 0)
            self.send(3, self.me, 1)
            self.send(1, self.me, 1)
            self.send(4, self.me, 0)

        def mid(self):
            self.c[0].wait_recv()
            self.send(2, (self.me + 3) % 4, 0)
            self.c[3].wait_recv()
            self.send(5, (self.me + 1) % 4, 1)

        def finish(self):
            for slot in (1, 4, 2, 5):
                self.c[slot].wait_recv()

    def quarter(half, part):
        return pl.ds(half * 32 + part * 16, 16)

    def along_x(ref, half):
        return lambda at, part: ref.at[at, :, quarter(half, part), :]

    def along_y(ref, half):
        return lambda at, part: ref.at[:, at, quarter(half, part), :]

    def in_x(ref, half):
        return lambda at, part: ref.at[at, y, quarter(half, part), :]

    def in_y(ref, half):
        return lambda at, part: ref.at[x, at, quarter(half, part), :]

    class Both:
        def __init__(self, *rings):
            self.rings = rings

        def start(self):
            for ring in self.rings:
                ring.start()

        def mid(self):
            for ring in self.rings:
                ring.mid()

        def finish(self):
            for ring in self.rings:
                ring.finish()

    def scatter(v):
        ref = du.at[v]
        return (
            Both(Scatter4(along_x(ref, 0), x, x_next, x_prev, rs_buf.at[v, 0]),
                 Scatter4(along_y(ref, 1), y, y_next, y_prev, rs_buf.at[v, 1])),
            Both(Scatter4(in_y(ref, 0), y, y_next, y_prev, rs_small.at[v, 0]),
                 Scatter4(in_x(ref, 1), x, x_next, x_prev, rs_small.at[v, 1])))

    def gather(ref):
        return (
            Both(Gather4(in_y(ref, 0), y, y_next, y_prev),
                 Gather4(in_x(ref, 1), x, x_next, x_prev)),
            Both(Gather4(along_x(ref, 0), x, x_next, x_prev),
                 Gather4(along_y(ref, 1), y, y_next, y_prev)))

    hops = (4, 3, 3, 2, 2, 1, 1)
    split = 2
    units = len(hops) * split
    back = 2 * split

    class ScatterZ:
        def __init__(self):
            self.c = {}

        def view(self, dest, way, i):
            part = i // split % 2 ^ way
            return dc_half.at[dest, pl.ds(part * 128 + i % split * (128 // split), 128 // split), :]

        def step(self, i):
            for way in (0, 1):
                hop = hops[i // split]
                spot = self.view((me_z + (n_z - hop if way else hop)) % n_z, way, i)
                if i >= back:
                    self.c[way, i - back].wait_recv()
                    add_to(spot, z_buf[way, i - back])
                self.c[way, i] = send(spot, z_buf.at[way, i], z_prev if way else z_next)

        def finish(self):
            for i in range(units - back, units):
                for way in (0, 1):
                    self.c[way, i].wait_recv()
                    add_to(self.view(me_z, way, i), z_buf[way, i])

    class GatherZ:
        def __init__(self):
            self.c = {}
            self.p = []

        def view(self, owner, way, i):
            part = i // split % 2 ^ way
            return agw.at[core * n_z + owner, pl.ds(part * 64 + i % split * (64 // split), 64 // split), :]

        def relay(self, way, i):
            self.c[way, i].wait_recv()
            far = i // split // 2 + 1
            spot = self.view((me_z + (far if way else n_z - far)) % n_z, way, i)
            return spot

        def step(self, i):
            for way in (0, 1):
                if i >= back:
                    spot = self.relay(way, i - back)
                else:
                    spot = self.view(me_z, way, i)
                self.c[way, i] = send(spot, spot, z_prev if way else z_next)
                if i >= back:
                    self.p.append(send(spot, spot, partner))

        def own(self):
            spot = agw.at[core * n_z + me_z]
            self.p.append(send(spot, spot, partner))

        def finish(self):
            for i in range(units - back, units):
                for way in (0, 1):
                    spot = self.relay(way, i)
                    self.p.append(send(spot, spot, partner))

    rings = [scatter(0), scatter(1)]

    step_m, step_w = 256, 512

    def first_pass(v):
        def step(i, cols):
            at = pl.ds(pl.multiple_of(i * step_m, step_m), step_m)
            glob = pl.ds(pl.multiple_of(v * clips + i * step_m, step_m), step_m)
            unit, _ = normalized(embeds[v][at, :].astype(F32))
            ub = unit.astype(BF16)
            unit_b[glob, :] = ub
            den = jnp.zeros((step_m, 128), F32)
            cols = list(cols)
            for k in range(protos // step_w):
                score = lax.dot_general(
                    ub, proto_b[k * step_w:(k + 1) * step_w, :],
                    (((1,), (1,)), ((), ())), preferred_element_type=F32)
                soft = jnp.exp(score * 10.0)
                code = soft * soft
                table[glob, k * step_w:(k + 1) * step_w] = code
                for j in range(step_w // 128):
                    den = den + soft[:, chunk(j)]
                    c = k * (step_w // 128) + j
                    cols[c] = cols[c] + fold8(code[:, chunk(j)])
            for j in range(step_m // 128):
                den_recv[me_p, pl.ds(v * view_blocks + i * (step_m // 128) + j, 1), :] = lane_sums(den[chunk(j), :])
            return tuple(cols)

        return lax.fori_loop(0, clips // step_m, step, (zero,) * lane_chunks)

    def cols_pass(v):
        def step(i, cols):
            at = pl.ds(pl.multiple_of(v * clips + i * 64, 64), 64)
            s = clip_b[at, :]
            return tuple(cols[c] + fold8(table[at, chunk(c)] * s) for c in range(lane_chunks))

        return lax.fori_loop(0, clips // 64, step, (zero,) * lane_chunks)

    def rows_pass(it, v):
        def step(i, carry):
            for j in range(2):
                block = 2 * i + j
                at = pl.ds(pl.multiple_of(v * clips + block * 128, 128), 128)
                acc = jnp.zeros((128, 128), F32)
                for c in range(lane_chunks):
                    acc = acc + table[at, chunk(c)] * scale[v, c:c + 1, :]
                row_recv[it, v, me_p, pl.ds(block, 1), :] = lane_sums(acc)
            return carry

        lax.fori_loop(0, view_blocks // 2, step, 0)
        return start_all(row_recv.at[it, v], me_p, n_p, p_id, row_send.at[it, v], row_sem.at[it, v])

    def wait_all(copies):
        for copy in copies:
            copy.wait_recv()
        sends.extend(copies)

    def pair_start(it, v, copies):
        wait_all(copies)
        pair = col_pair.at[it, v]
        pair[core] = total_of(col_z.at[it, v], n_z)
        copy = remote(pair.at[core], pair.at[core], colp_send.at[it, v], colp_sem.at[it, v], partner)
        copy.start()
        return copy

    sends = []
    z_copies = [None, None]
    row_copies = [None, None]
    z_cols = first_pass(0)
    pl.semaphore_wait(barrier, n_p - 1 + 2 * n_z - 1)
    z_copies[0] = put_cols(0, 0, z_cols)
    z_copies[1] = put_cols(0, 1, first_pass(1))
    den_copies = start_all(den_recv, me_p, n_p, p_id, den_send, den_sem)

    def transpose_unit(i, carry):
        at = pl.ds(pl.multiple_of(i * 128, 128), 128)
        unit_t[:, at] = unit_b[at, :].astype(F32).T.astype(BF16)
        return carry

    lax.fori_loop(0, row_blocks, transpose_unit, 0)

    def grad_pass(v):
        w = 1 - v

        def step(i, carry):
            mine = pl.ds(pl.multiple_of(v * clips + i * 64, 64), 64)
            other = pl.ds(pl.multiple_of(w * clips + i * 64, 64), 64)
            soft_scale = soft_b[mine, :]
            code_scale = code_b[other, :]
            for c in range(lane_chunks):
                e = table[mine, chunk(c)]
                code = table[other, chunk(c)] * scale[w, c:c + 1, :] * code_scale
                grads[mine, chunk(c)] = (e * lax.rsqrt(e) * soft_scale - code).astype(BF16)
            return carry

        lax.fori_loop(0, clips // 64, step, 0)

    def du_dot(v):
        def step(i, carry):
            at = pl.ds(pl.multiple_of(v * clips + i * 512, 512), 512)
            out = jnp.dot(grads[at, :], proto_b[...], preferred_element_type=F32)
            du[v, pl.ds(2 * i, 2)] = out.reshape(2, 4, 64, width)
            return carry

        lax.fori_loop(0, clips // 512, step, 0)

    for it in range(ITERS):
        pairs = [pair_start(it, v, z_copies[v]) for v in range(2)]
        for v in range(2):
            wait_all([pairs[v]])
            scale[v] = 1.0 / (protos_all * (col_pair[it, v, 0] + col_pair[it, v, 1]))
            row_copies[v] = rows_pass(it, v)
        if it == 0:
            wait_all(den_copies)
            soft = 10.0 / total_of(den_recv, n_p)
            for v in range(2):
                spread(soft[v * view_blocks:(v + 1) * view_blocks], v, soft_b)
        for v in range(2):
            wait_all(row_copies[v])
            row_sum = total_of(row_recv.at[it, v], n_p)
            if it < ITERS - 1:
                spread(1.0 / (clips_all * row_sum), v, clip_b)
                z_copies[v] = put_cols(it + 1, v, cols_pass(v))
            else:
                spread(10.0 / row_sum, v, code_b)
                grad_pass(1 - v)
                if v == 0:
                    du_dot(1)
                    rings[1][0].start()

    def project(grad, raw):
        unit, inverse = normalized(raw)
        along = jnp.sum(unit * grad, axis=-1, keepdims=True)
        return (grad - unit * along) * inverse

    def lanes_square(block):
        sq = block * block
        return jnp.sum(sq[:, :128] + sq[:, 128:], axis=0, keepdims=True)

    theirs = (1 - core) * n_z

    def pair_piece(i):
        return remote(
            dct.at[pl.ds(theirs + 2 * i, 2)], dc_pair.at[pl.ds(2 * i, 2)],
            pair_out.at[i], pair_in.at[i], partner)

    def dc_dot(first_chunk, sending):
        def step(i, carry):
            c = first_chunk + 2 * i
            at = pl.ds(pl.multiple_of(c * 128, 256), 256)
            out = jnp.dot(unit_t[...], grads[:, at], preferred_element_type=F32)
            dct[c] = out[:, :128]
            dct[c + 1] = out[:, 128:]
            if sending:
                pair_piece(i).start()
            return carry

        lax.fori_loop(0, n_z // 2, step, 0)

    outs = (slow_out, fast_out)
    gathers = [gather(out) for out in outs]
    zs, zg = ScatterZ(), GatherZ()

    def own_rows(v):
        raw = embeds[v][pl.ds(pl.multiple_of(me_p * 64, 64), 64), :].astype(F32)
        own = project(du[v, x, y], raw)
        outs[v][x, y] = own
        gathers[v][0].start()
        return lanes_square(own)

    rings[1][0].mid()
    dc_dot(theirs, True)
    dc_dot(core * n_z, False)
    for i in range(n_z // 2):
        pair_piece(i).wait_recv()
        for j in (2 * i, 2 * i + 1):
            dc_half[j] = dct[core * n_z + j] + dc_pair[j]
    for i in range(back):
        zs.step(i)
    du_dot(0)
    rings[0][0].start()
    rings[1][0].finish()
    rings[1][1].start()
    zs.step(4)
    zs.step(5)
    rings[1][1].mid()
    zs.step(6)
    rings[0][0].mid()
    zs.step(7)
    rings[1][1].finish()
    square_x = own_rows(1)
    zs.step(8)
    zs.step(9)
    gathers[1][0].mid()
    rings[0][0].finish()
    rings[0][1].start()
    zs.step(10)
    zs.step(11)
    gathers[1][0].finish()
    gathers[1][1].start()
    rings[0][1].mid()
    zs.step(12)
    zs.step(13)
    zs.finish()
    mine = core * n_z + me_z
    dw_own = project(dc_half[me_z].T, proto_ref[pl.ds(pl.multiple_of(mine * 128, 128), 128), :])
    agw[mine] = dw_own
    for i in range(back):
        zg.step(i)
    zg.own()
    rings[0][1].finish()
    square_x = square_x + own_rows(0)
    sq_p[me_p, 0:1, :] = lanes_square(dw_own)
    sq_p[me_p, 1:2, :] = square_x
    sq_p[me_p, 2:8, :] = jnp.zeros((6, 128), F32)
    sq_copies = start_all(sq_p, me_p, n_p, p_id, send_sem, sqp_sem)
    gathers[1][1].mid()
    zg.step(4)
    zg.step(5)
    gathers[0][0].mid()
    zg.step(6)
    zg.step(7)
    gathers[0][0].finish()
    gathers[0][1].start()
    zg.step(8)
    zg.step(9)
    zg.step(10)
    gathers[0][1].mid()
    zg.step(11)
    wait_all(sq_copies)
    sq_z[batch_me] = total_of(sq_p, n_p)
    sq_copies = start_all(sq_z, batch_me, 2 * n_z, b_id, sqz_send, sqz_sem)
    zg.step(12)
    zg.step(13)
    gathers[1][1].finish()
    gathers[0][1].finish()
    zg.finish()
    wait_all(sq_copies)
    square = jnp.sum(total_of(sq_z, 2 * n_z), axis=1, keepdims=True)
    entries = float(protos_all * width), float(2 * clips_all * width)
    for i, out in enumerate((wf_ref, xf_ref)):
        out[...] = jnp.broadcast_to(
            lax.rsqrt(square[i:i + 1, :] / entries[i] + NORM_EPS), (8, width))
    for copy in zg.p:
        copy.wait_recv()
    for i in range(n_z // 2):
        pair_piece(i).wait_send()
    for copy in pending + sends:
        copy.wait_send()


def body(slow_embed, fast_embed, prototypes):
    clips, width = slow_embed.shape
    protos = prototypes.shape[0]
    n_b = lax.axis_size("batch")
    n_p = lax.axis_size("proto")
    n_z = n_b // 2
    rows = 2 * clips
    DMA = pltpu.SemaphoreType.DMA
    vmem = pltpu.VMEM
    lane_chunks = protos // 128
    row_blocks = rows // 128
    scratch = [
        vmem((rows, protos), F32),
        vmem((rows, protos), BF16),
        vmem((rows, width), BF16),
        vmem((width, rows), BF16),
        vmem((protos, width), BF16),
        vmem((2, lane_chunks, 128), F32),
        vmem((rows, 128), F32),
        vmem((rows, 128), F32),
        vmem((rows, 128), F32),
        vmem((2, 4, 4, 64, width), F32),
        vmem((lane_chunks, width, 128), F32),
        vmem((n_z, width, 128), F32),
        vmem((n_z, width, 128), F32),
        vmem((2, 2, 6, 4, 16, width), F32),
        vmem((2, 2, 6, 16, width), F32),
        vmem((2, 14, 64, 128), F32),
        vmem((ITERS, 2, n_z, lane_chunks, 128), F32),
        vmem((ITERS, 2, 2, lane_chunks, 128), F32),
        vmem((ITERS, 2, n_p, row_blocks // 2, 128), F32),
        vmem((n_p, row_blocks, 128), F32),
        vmem((n_p, 8, 128), F32),
        vmem((n_b, 8, 128), F32),
        DMA((16,)), DMA((ITERS, 2, n_z)), DMA((ITERS, 2, n_z)), DMA((ITERS, 2)), DMA((ITERS, 2)),
        DMA((ITERS, 2, n_p)), DMA((ITERS, 2, n_p)),
        DMA((n_p,)), DMA((n_p,)),
        DMA((n_p,)), DMA((n_b,)), DMA((n_b,)), DMA((n_z // 2,)), DMA((n_z // 2,)),
        DMA((COPIES,)), DMA((COPIES,)),
    ]
    whole = pl.BlockSpec(memory_space=pltpu.VMEM)
    dw, slow, fast, dw_factor, dx_factor = pl.pallas_call(
        functools.partial(kernel, (clips, protos, width, n_z, n_p)),
        out_shape=(
            vmem((lane_chunks, 128, width), F32),
            vmem((4, 4, 64, width), F32),
            vmem((4, 4, 64, width), F32),
            vmem((8, width), F32),
            vmem((8, width), F32),
        ),
        in_specs=[whole] * 3,
        out_specs=(whole,) * 5,
        scratch_shapes=scratch,
        compiler_params=pltpu.CompilerParams(
            collective_id=0, has_side_effects=True, vmem_limit_bytes=56 * 2**20),
        name="swav",
    )(slow_embed, fast_embed, prototypes)

    def scaled(array, factor, rows):
        return (array.reshape(rows // 8, 8, width) * factor).reshape(rows, width)

    return (
        scaled(dw, dw_factor, protos),
        scaled(slow, dx_factor, clips),
        scaled(fast, dx_factor, clips),
    )


def solution(mesh):
    placed = (P("batch", None), P("batch", None), P("proto", None))
    return jax.shard_map(
        body,
        mesh=mesh,
        in_specs=placed,
        out_specs=(P("proto", None), P("batch", None), P("batch", None)),
        check_vma=False,
    )
```

time: 113 us -> 118 us (1.044)
  Pallas kernels: 107 us -> 114 us
  other arithmetic: 4.66 us -> 2.92 us
    pallas_call x1, Pallas kernels: 107 us -> 114 us  [body(): pl.pallas_call(functools.partial(kernel, (clips, protos, width, n_z, n_p)...]
    mul x2, other arithmetic: 4.66 us -> 2.92 us  [scaled(): return (array.reshape(rows // 8, 8, width) * factor).reshape(rows, width)]
where the time goes in v4:
time: 118 us
  Pallas kernels  114 us (97%)
  other arithmetic  2.92 us (2%)
    pallas_call x1, Pallas kernels, body(): pl.pallas_call(functools.partial(kernel, (clips, protos, width, n_z, n_p)...  114 us
    mul x2, other arithmetic, scaled(): return (array.reshape(rows // 8, 8, width) * factor).reshape(rows, width)  2.92 us

profile of v4, /device:TPU:1, one launch (start us, length us, event | category | flops | bytes accessed | tf_op | source)
XLA Modules:
  0.0 118.0 jit_solution(3040019892523897954)
XLA Ops:
  0.6 114.5 %swav.1 = (f32[16,128,256]{2,1,0:T(8,128)S(1)}, f32[4,4,64,256]{3,2,1,0:T(8,128)S(1)}, f32[4,4,64,256]{3,2,1,0:T(8,128)S(1)}, f32[8,256]{1,0:T(8,128)S(1)}, f32[8,256]{1,0:T(8,128)S(1)}) custom-call(bf16[1024,256]{1,0:T(8,128)(2,1)} %slow_ref.1, bf16[1024,256]{1,0:T(8,128)(2,1)} %fast_ref.1, f32[2048,256]{1,0:T(8,128)} %proto_ref.1), custom_call_target="tpu_custom_call" | custom-call | tf_op jit(solution)/shard_map/swav/pallas_call | solution.py:593
  115.1 1.5 %bitcast_multiply_fusion = f32[2048,256]{1,0:T(8,128)} fusion(f32[16,128,256]{2,1,0:T(8,128)S(1)} %get-tuple-element.8, f32[8,256]{1,0:T(8,128)S(1)} %get-tuple-element.9), kind=kLoop, calls=%fused_computation | loop fusion | flops 524288 | bytes 4202496 | tf_op jit(solution)/shard_map/mul | solution.py:611
  116.6 1.5 %bitcast_multiply_fusion.1 = (f32[1024,256]{1,0:T(8,128)}, f32[1024,256]{1,0:T(8,128)}) fusion(f32[4,4,64,256]{3,2,1,0:T(8,128)S(1)} %get-tuple-element.12, f32[8,256]{1,0:T(8,128)S(1)} %get-tuple-element.11, f32[4,4,64,256]{3,2,1,0:T(8,128)S(1)} %get-tuple-element.10), kind=kLoop, calls=%fused_computation.1 | loop fusion | flops 524288 | bytes 4202496 | tf_op jit(solution)/shard_map/mul | solution.py:611

commit v5 on v4

--- a/solution.py
+++ b/solution.py
@@ -29,7 +29,7 @@
 def kernel(
     dims,
     slow_ref, fast_ref, proto_ref,
-    agw, slow_out, fast_out, wf_ref, xf_ref,
+    agw, agx, wf_ref, xf_ref,
     table, grads, unit_b, unit_t, proto_b, scale, clip_b, soft_b, code_b,
     du, dct, dc_pair, dc_half, rs_buf, rs_small, z_buf,
     col_z, col_pair, row_recv, den_recv, sq_p, sq_z,
@@ -190,7 +190,7 @@
                 self.c[slot].wait_recv()
 
     def quarter(half, part):
-        return pl.ds(half * 32 + part * 16, 16)
+        return pl.ds(half * 64 + part * 32, 32)
 
     def along_x(ref, half):
         return lambda at, part: ref.at[at, :, quarter(half, part), :]
@@ -220,13 +220,12 @@
             for ring in self.rings:
                 ring.finish()
 
-    def scatter(v):
-        ref = du.at[v]
+    def scatter(ref):
         return (
-            Both(Scatter4(along_x(ref, 0), x, x_next, x_prev, rs_buf.at[v, 0]),
-                 Scatter4(along_y(ref, 1), y, y_next, y_prev, rs_buf.at[v, 1])),
-            Both(Scatter4(in_y(ref, 0), y, y_next, y_prev, rs_small.at[v, 0]),
-                 Scatter4(in_x(ref, 1), x, x_next, x_prev, rs_small.at[v, 1])))
+            Both(Scatter4(along_x(ref, 0), x, x_next, x_prev, rs_buf.at[0]),
+                 Scatter4(along_y(ref, 1), y, y_next, y_prev, rs_buf.at[1])),
+            Both(Scatter4(in_y(ref, 0), y, y_next, y_prev, rs_small.at[0]),
+                 Scatter4(in_x(ref, 1), x, x_next, x_prev, rs_small.at[1])))
 
     def gather(ref):
         return (
@@ -236,7 +235,7 @@
                  Gather4(along_y(ref, 1), y, y_next, y_prev)))
 
     hops = (4, 3, 3, 2, 2, 1, 1)
-    split = 2
+    split = 1
     units = len(hops) * split
     back = 2 * split
 
@@ -298,7 +297,6 @@
                     spot = self.relay(way, i)
                     self.p.append(send(spot, spot, partner))
 
-    rings = [scatter(0), scatter(1)]
 
     step_m, step_w = 256, 512
 
@@ -379,30 +377,39 @@
 
     lax.fori_loop(0, row_blocks, transpose_unit, 0)
 
-    def grad_pass(v):
+    def grad_rows(v, first, count):
         w = 1 - v
-
+        mine = pl.ds(pl.multiple_of(v * clips + first, count), count)
+        other = pl.ds(pl.multiple_of(w * clips + first, count), count)
+        soft_scale = soft_b[mine, :]
+        code_scale = code_b[other, :]
+        for c in range(lane_chunks):
+            e = table[mine, chunk(c)]
+            code = table[other, chunk(c)] * scale[w, c:c + 1, :] * code_scale
+            grads[mine, chunk(c)] = (e * lax.rsqrt(e) * soft_scale - code).astype(BF16)
+
+    def du_rows(v, i):
+        at = pl.ds(pl.multiple_of(v * clips + i * 256, 256), 256)
+        out = jnp.dot(grads[at, :], proto_b[...], preferred_element_type=F32)
+        owner = v * (n_p // 2) + 2 * i
+        du[owner // 4, pl.ds(owner % 4, 2)] = out.reshape(2, 128, width)
+
+    def grad_pass(v, dots=None):
         def step(i, carry):
-            mine = pl.ds(pl.multiple_of(v * clips + i * 64, 64), 64)
-            other = pl.ds(pl.multiple_of(w * clips + i * 64, 64), 64)
-            soft_scale = soft_b[mine, :]
-            code_scale = code_b[other, :]
-            for c in range(lane_chunks):
-                e = table[mine, chunk(c)]
-                code = table[other, chunk(c)] * scale[w, c:c + 1, :] * code_scale
-                grads[mine, chunk(c)] = (e * lax.rsqrt(e) * soft_scale - code).astype(BF16)
+            if dots is not None:
+                du_rows(dots, i)
+            for j in range(4):
+                grad_rows(v, i * 256 + j * 64, 64)
             return carry
 
-        lax.fori_loop(0, clips // 64, step, 0)
+        lax.fori_loop(0, clips // 256, step, 0)
 
     def du_dot(v):
         def step(i, carry):
-            at = pl.ds(pl.multiple_of(v * clips + i * 512, 512), 512)
-            out = jnp.dot(grads[at, :], proto_b[...], preferred_element_type=F32)
-            du[v, pl.ds(2 * i, 2)] = out.reshape(2, 4, 64, width)
+            du_rows(v, i)
             return carry
 
-        lax.fori_loop(0, clips // 512, step, 0)
+        lax.fori_loop(0, clips // 256, step, 0)
 
     for it in range(ITERS):
         pairs = [pair_start(it, v, z_copies[v]) for v in range(2)]
@@ -423,10 +430,7 @@
                 z_copies[v] = put_cols(it + 1, v, cols_pass(v))
             else:
                 spread(10.0 / row_sum, v, code_b)
-                grad_pass(1 - v)
-                if v == 0:
-                    du_dot(1)
-                    rings[1][0].start()
+                grad_pass(1 - v, 1 if v == 1 else None)
 
     def project(grad, raw):
         unit, inverse = normalized(raw)
@@ -457,83 +461,57 @@
 
         lax.fori_loop(0, n_z // 2, step, 0)
 
-    outs = (slow_out, fast_out)
-    gathers = [gather(out) for out in outs]
+    r1, r2 = scatter(du)
+    g1, g2 = gather(agx)
     zs, zg = ScatterZ(), GatherZ()
-
-    def own_rows(v):
-        raw = embeds[v][pl.ds(pl.multiple_of(me_p * 64, 64), 64), :].astype(F32)
-        own = project(du[v, x, y], raw)
-        outs[v][x, y] = own
-        gathers[v][0].start()
-        return lanes_square(own)
-
-    rings[1][0].mid()
+    du_dot(0)
+    r1.start()
     dc_dot(theirs, True)
     dc_dot(core * n_z, False)
     for i in range(n_z // 2):
         pair_piece(i).wait_recv()
         for j in (2 * i, 2 * i + 1):
             dc_half[j] = dct[core * n_z + j] + dc_pair[j]
-    for i in range(back):
-        zs.step(i)
-    du_dot(0)
-    rings[0][0].start()
-    rings[1][0].finish()
-    rings[1][1].start()
+    zs.step(0)
+    zs.step(1)
+    r1.mid()
+    zs.step(2)
+    zs.step(3)
     zs.step(4)
+    r1.finish()
+    r2.start()
     zs.step(5)
-    rings[1][1].mid()
     zs.step(6)
-    rings[0][0].mid()
-    zs.step(7)
-    rings[1][1].finish()
-    square_x = own_rows(1)
-    zs.step(8)
-    zs.step(9)
-    gathers[1][0].mid()
-    rings[0][0].finish()
-    rings[0][1].start()
-    zs.step(10)
-    zs.step(11)
-    gathers[1][0].finish()
-    gathers[1][1].start()
-    rings[0][1].mid()
-    zs.step(12)
-    zs.step(13)
+    r2.mid()
+    r2.finish()
+    at = pl.ds(pl.multiple_of((me_p % view_blocks) * 128, 128), 128)
+    raw = jnp.where(me_p < view_blocks, slow_ref[at, :].astype(F32), fast_ref[at, :].astype(F32))
+    dx_own = project(du[x, y], raw)
+    agx[x, y] = dx_own
+    g1.start()
     zs.finish()
     mine = core * n_z + me_z
     dw_own = project(dc_half[me_z].T, proto_ref[pl.ds(pl.multiple_of(mine * 128, 128), 128), :])
     agw[mine] = dw_own
-    for i in range(back):
-        zg.step(i)
+    zg.step(0)
+    zg.step(1)
     zg.own()
-    rings[0][1].finish()
-    square_x = square_x + own_rows(0)
     sq_p[me_p, 0:1, :] = lanes_square(dw_own)
-    sq_p[me_p, 1:2, :] = square_x
+    sq_p[me_p, 1:2, :] = lanes_square(dx_own)
     sq_p[me_p, 2:8, :] = jnp.zeros((6, 128), F32)
     sq_copies = start_all(sq_p, me_p, n_p, p_id, send_sem, sqp_sem)
-    gathers[1][1].mid()
+    g1.mid()
+    zg.step(2)
+    g1.finish()
+    g2.start()
+    zg.step(3)
     zg.step(4)
-    zg.step(5)
-    gathers[0][0].mid()
-    zg.step(6)
-    zg.step(7)
-    gathers[0][0].finish()
-    gathers[0][1].start()
-    zg.step(8)
-    zg.step(9)
-    zg.step(10)
-    gathers[0][1].mid()
-    zg.step(11)
     wait_all(sq_copies)
     sq_z[batch_me] = total_of(sq_p, n_p)
     sq_copies = start_all(sq_z, batch_me, 2 * n_z, b_id, sqz_send, sqz_sem)
-    zg.step(12)
-    zg.step(13)
-    gathers[1][1].finish()
-    gathers[0][1].finish()
+    zg.step(5)
+    g2.mid()
+    zg.step(6)
     zg.finish()
     wait_all(sq_copies)
     square = jnp.sum(total_of(sq_z, 2 * n_z), axis=1, keepdims=True)
@@ -541,6 +519,7 @@
     for i, out in enumerate((wf_ref, xf_ref)):
         out[...] = jnp.broadcast_to(
             lax.rsqrt(square[i:i + 1, :] / entries[i] + NORM_EPS), (8, width))
+    g2.finish()
     for copy in zg.p:
         copy.wait_recv()
     for i in range(n_z // 2):
@@ -570,13 +549,13 @@
         vmem((rows, 128), F32),
         vmem((rows, 128), F32),
         vmem((rows, 128), F32),
-        vmem((2, 4, 4, 64, width), F32),
+        vmem((4, 4, 128, width), F32),
         vmem((lane_chunks, width, 128), F32),
         vmem((n_z, width, 128), F32),
         vmem((n_z, width, 128), F32),
-        vmem((2, 2, 6, 4, 16, width), F32),
-        vmem((2, 2, 6, 16, width), F32),
-        vmem((2, 14, 64, 128), F32),
+        vmem((2, 6, 4, 32, width), F32),
+        vmem((2, 6, 32, width), F32),
+        vmem((2, 7, 128, 128), F32),
         vmem((ITERS, 2, n_z, lane_chunks, 128), F32),
         vmem((ITERS, 2, 2, lane_chunks, 128), F32),
         vmem((ITERS, 2, n_p, row_blocks // 2, 128), F32),
@@ -590,17 +569,16 @@
         DMA((COPIES,)), DMA((COPIES,)),
     ]
     whole = pl.BlockSpec(memory_space=pltpu.VMEM)
-    dw, slow, fast, dw_factor, dx_factor = pl.pallas_call(
+    dw, dx, dw_factor, dx_factor = pl.pallas_call(
         functools.partial(kernel, (clips, protos, width, n_z, n_p)),
         out_shape=(
             vmem((lane_chunks, 128, width), F32),
-            vmem((4, 4, 64, width), F32),
-            vmem((4, 4, 64, width), F32),
+            vmem((4, 4, 128, width), F32),
             vmem((8, width), F32),
             vmem((8, width), F32),
         ),
         in_specs=[whole] * 3,
-        out_specs=(whole,) * 5,
+        out_specs=(whole,) * 4,
         scratch_shapes=scratch,
         compiler_params=pltpu.CompilerParams(
             collective_id=0, has_side_effects=True, vmem_limit_bytes=56 * 2**20),
@@ -612,8 +590,8 @@
 
     return (
         scaled(dw, dw_factor, protos),
-        scaled(slow, dx_factor, clips),
-        scaled(fast, dx_factor, clips),
+        scaled(dx[:2], dx_factor, clips),
+        scaled(dx[2:], dx_factor, clips),
     )
 
 

time: 118 us -> 111 us (0.941)
  Pallas kernels: 114 us -> 107 us
    pallas_call x1, Pallas kernels: 114 us -> 107 us  [body(): pl.pallas_call(functools.partial(kernel, (clips, protos, width, n_z, n_p)...]
where the time goes in v5:
time: 111 us
  Pallas kernels  107 us (96%)
  other arithmetic  2.92 us (3%)
    pallas_call x1, Pallas kernels, body(): pl.pallas_call(functools.partial(kernel, (clips, protos, width, n_z, n_p)...  107 us
    mul x2, other arithmetic, scaled(): return (array.reshape(rows // 8, 8, width) * factor).reshape(rows, width)  2.92 us

profile of v5, /device:TPU:1, one launch (start us, length us, event | category | flops | bytes accessed | tf_op | source)
XLA Modules:
  0.0 110.6 jit_solution(8662631786878535018)
XLA Ops:
  0.6 106.9 %swav.1 = (f32[16,128,256]{2,1,0:T(8,128)S(1)}, f32[4,4,128,256]{3,2,1,0:T(8,128)S(1)}, f32[8,256]{1,0:T(8,128)S(1)}, f32[8,256]{1,0:T(8,128)S(1)}) custom-call(bf16[1024,256]{1,0:T(8,128)(2,1)} %slow_ref.1, bf16[1024,256]{1,0:T(8,128)(2,1)} %fast_ref.1, f32[2048,256]{1,0:T(8,128)} %proto_ref.1), custom_call_target="tpu_custom_call" | custom-call | tf_op jit(solution)/shard_map/swav/pallas_call | solution.py:572
  107.6 1.5 %bitcast_multiply_fusion = f32[2048,256]{1,0:T(8,128)} fusion(f32[16,128,256]{2,1,0:T(8,128)S(1)} %get-tuple-element.7, f32[8,256]{1,0:T(8,128)S(1)} %get-tuple-element.8), kind=kLoop, calls=%fused_computation | loop fusion | flops 524288 | bytes 4202496 | tf_op jit(solution)/shard_map/mul | solution.py:589
  109.0 0.1 fusion
  109.2 1.5 %bitcast_multiply_fusion.1 = (f32[1024,256]{1,0:T(8,128)}, f32[1024,256]{1,0:T(8,128)}) fusion(f32[2,4,128,256]{3,2,1,0:T(8,128)S(1)} %get-tuple-element.11, f32[8,256]{1,0:T(8,128)S(1)} %get-tuple-element.10, f32[2,4,128,256]{3,2,1,0:T(8,128)S(1)} %get-tuple-element.12), kind=kLoop, calls=%fused_computation.1 | loop fusion | flops 524288 | bytes 4202496 | tf_op jit(solution)/shard_map/mul | solution.py:589

commit v6 on v5

--- a/solution.py
+++ b/solution.py
@@ -9,6 +9,7 @@
 
 ITERS = 3
 COPIES = 192
+EXPONENT = 10.0 * 1.4426950408889634
 NORM_EPS = 1e-06
 MESH = pl.DeviceIdType.MESH
 F32 = jnp.float32
@@ -298,7 +299,7 @@
                     self.p.append(send(spot, spot, partner))
 
 
-    step_m, step_w = 256, 512
+    step_m, step_w = 512, 512
 
     def first_pass(v):
         def step(i, cols):
@@ -307,21 +308,17 @@
             unit, _ = normalized(embeds[v][at, :].astype(F32))
             ub = unit.astype(BF16)
             unit_b[glob, :] = ub
-            den = jnp.zeros((step_m, 128), F32)
             cols = list(cols)
             for k in range(protos // step_w):
                 score = lax.dot_general(
                     ub, proto_b[k * step_w:(k + 1) * step_w, :],
                     (((1,), (1,)), ((), ())), preferred_element_type=F32)
-                soft = jnp.exp(score * 10.0)
+                soft = jnp.exp2(score * EXPONENT)
                 code = soft * soft
                 table[glob, k * step_w:(k + 1) * step_w] = code
                 for j in range(step_w // 128):
-                    den = den + soft[:, chunk(j)]
                     c = k * (step_w // 128) + j
                     cols[c] = cols[c] + fold8(code[:, chunk(j)])
-            for j in range(step_m // 128):
-                den_recv[me_p, pl.ds(v * view_blocks + i * (step_m // 128) + j, 1), :] = lane_sums(den[chunk(j), :])
             return tuple(cols)
 
         return lax.fori_loop(0, clips // step_m, step, (zero,) * lane_chunks)
@@ -368,14 +365,24 @@
     pl.semaphore_wait(barrier, n_p - 1 + 2 * n_z - 1)
     z_copies[0] = put_cols(0, 0, z_cols)
     z_copies[1] = put_cols(0, 1, first_pass(1))
+
+    def soft_totals(i, carry):
+        at = pl.ds(pl.multiple_of(i * 128, 128), 128)
+        acc = jnp.zeros((128, 128), F32)
+        for c in range(lane_chunks):
+            e = table[at, chunk(c)]
+            acc = acc + e * lax.rsqrt(e)
+        den_recv[me_p, pl.ds(i, 1), :] = lane_sums(acc)
+        return carry
+
+    lax.fori_loop(0, row_blocks, soft_totals, 0)
     den_copies = start_all(den_recv, me_p, n_p, p_id, den_send, den_sem)
 
     def transpose_unit(i, carry):
         at = pl.ds(pl.multiple_of(i * 128, 128), 128)
-        unit_t[:, at] = unit_b[at, :].astype(F32).T.astype(BF16)
+        unit_t[i] = unit_b[at, :].astype(F32).T.astype(BF16)
         return carry
 
-    lax.fori_loop(0, row_blocks, transpose_unit, 0)
 
     def grad_rows(v, first, count):
         w = 1 - v
@@ -386,18 +393,17 @@
         for c in range(lane_chunks):
             e = table[mine, chunk(c)]
             code = table[other, chunk(c)] * scale[w, c:c + 1, :] * code_scale
-            grads[mine, chunk(c)] = (e * lax.rsqrt(e) * soft_scale - code).astype(BF16)
+            grads[c, mine, :] = (e * lax.rsqrt(e) * soft_scale - code).astype(BF16)
 
     def du_rows(v, i):
         at = pl.ds(pl.multiple_of(v * clips + i * 256, 256), 256)
-        out = jnp.dot(grads[at, :], proto_b[...], preferred_element_type=F32)
+        mine = jnp.concatenate([grads[c, at, :] for c in range(lane_chunks)], axis=1)
+        out = jnp.dot(mine, proto_b[...], preferred_element_type=F32)
         owner = v * (n_p // 2) + 2 * i
         du[owner // 4, pl.ds(owner % 4, 2)] = out.reshape(2, 128, width)
 
-    def grad_pass(v, dots=None):
+    def grad_pass(v):
         def step(i, carry):
-            if dots is not None:
-                du_rows(dots, i)
             for j in range(4):
                 grad_rows(v, i * 256 + j * 64, 64)
             return carry
@@ -418,6 +424,8 @@
             scale[v] = 1.0 / (protos_all * (col_pair[it, v, 0] + col_pair[it, v, 1]))
             row_copies[v] = rows_pass(it, v)
         if it == 0:
+            lax.fori_loop(0, row_blocks, transpose_unit, 0)
+        if it == 1:
             wait_all(den_copies)
             soft = 10.0 / total_of(den_recv, n_p)
             for v in range(2):
@@ -430,7 +438,9 @@
                 z_copies[v] = put_cols(it + 1, v, cols_pass(v))
             else:
                 spread(10.0 / row_sum, v, code_b)
-                grad_pass(1 - v, 1 if v == 1 else None)
+                grad_pass(1 - v)
+                if v == 0:
+                    du_dot(1)
 
     def project(grad, raw):
         unit, inverse = normalized(raw)
@@ -451,8 +461,9 @@
     def dc_dot(first_chunk, sending):
         def step(i, carry):
             c = first_chunk + 2 * i
-            at = pl.ds(pl.multiple_of(c * 128, 256), 256)
-            out = jnp.dot(unit_t[...], grads[:, at], preferred_element_type=F32)
+            units_t = jnp.concatenate([unit_t[j] for j in range(row_blocks)], axis=1)
+            pair = jnp.concatenate([grads[c], grads[c + 1]], axis=1)
+            out = jnp.dot(units_t, pair, preferred_element_type=F32)
             dct[c] = out[:, :128]
             dct[c + 1] = out[:, 128:]
             if sending:
@@ -541,9 +552,9 @@
     row_blocks = rows // 128
     scratch = [
         vmem((rows, protos), F32),
-        vmem((rows, protos), BF16),
+        vmem((lane_chunks, rows, 128), BF16),
         vmem((rows, width), BF16),
-        vmem((width, rows), BF16),
+        vmem((row_blocks, width, 128), BF16),
         vmem((protos, width), BF16),
         vmem((2, lane_chunks, 128), F32),
         vmem((rows, 128), F32),

time: 111 us -> 108 us (0.973)
  Pallas kernels: 107 us -> 104 us
    pallas_call x1, Pallas kernels: 107 us -> 104 us  [body(): pl.pallas_call(functools.partial(kernel, (clips, protos, width, n_z, n_p)...]
where the time goes in v6:
time: 108 us
  Pallas kernels  104 us (96%)
  other arithmetic  2.92 us (3%)
    pallas_call x1, Pallas kernels, body(): pl.pallas_call(functools.partial(kernel, (clips, protos, width, n_z, n_p)...  104 us
    mul x2, other arithmetic, scaled(): return (array.reshape(rows // 8, 8, width) * factor).reshape(rows, width)  2.92 us

profile of v6, /device:TPU:1, one launch (start us, length us, event | category | flops | bytes accessed | tf_op | source)
XLA Modules:
  0.0 108.0 jit_solution(4177413754079841457)
XLA Ops:
  0.6 104.3 %swav.1 = (f32[16,128,256]{2,1,0:T(8,128)S(1)}, f32[4,4,128,256]{3,2,1,0:T(8,128)S(1)}, f32[8,256]{1,0:T(8,128)S(1)}, f32[8,256]{1,0:T(8,128)S(1)}) custom-call(bf16[1024,256]{1,0:T(8,128)(2,1)} %slow_ref.1, bf16[1024,256]{1,0:T(8,128)(2,1)} %fast_ref.1, f32[2048,256]{1,0:T(8,128)} %proto_ref.1), custom_call_target="tpu_custom_call" | custom-call | tf_op jit(solution)/shard_map/swav/pallas_call | solution.py:583
  104.9 1.5 %bitcast_multiply_fusion = f32[2048,256]{1,0:T(8,128)} fusion(f32[16,128,256]{2,1,0:T(8,128)S(1)} %get-tuple-element.7, f32[8,256]{1,0:T(8,128)S(1)} %get-tuple-element.8), kind=kLoop, calls=%fused_computation | loop fusion | flops 524288 | bytes 4202496 | tf_op jit(solution)/shard_map/mul | solution.py:600
  106.4 0.1 fusion
  106.5 1.5 %bitcast_multiply_fusion.1 = (f32[1024,256]{1,0:T(8,128)}, f32[1024,256]{1,0:T(8,128)}) fusion(f32[2,4,128,256]{3,2,1,0:T(8,128)S(1)} %get-tuple-element.11, f32[8,256]{1,0:T(8,128)S(1)} %get-tuple-element.10, f32[2,4,128,256]{3,2,1,0:T(8,128)S(1)} %get-tuple-element.12), kind=kLoop, calls=%fused_computation.1 | loop fusion | flops 524288 | bytes 4202496 | tf_op jit(solution)/shard_map/mul | solution.py:600

commit v7 on v6

--- a/solution.py
+++ b/solution.py
@@ -8,7 +8,7 @@
 from jax.sharding import PartitionSpec as P
 
 ITERS = 3
-COPIES = 192
+COPIES = 51
 EXPONENT = 10.0 * 1.4426950408889634
 NORM_EPS = 1e-06
 MESH = pl.DeviceIdType.MESH
@@ -34,8 +34,8 @@
     table, grads, unit_b, unit_t, proto_b, scale, clip_b, soft_b, code_b,
     du, dct, dc_pair, dc_half, rs_buf, rs_small, z_buf,
     col_z, col_pair, row_recv, den_recv, sq_p, sq_z,
-    send_sem, col_send, col_sem, colp_send, colp_sem, row_send, row_sem, den_sem, den_send,
-    sqp_sem, sqz_sem, sqz_send, pair_out, pair_in, out_sem, in_sem,
+    col_send, col_sem, colp_send, colp_sem, row_send, row_sem, small_send, small_sem,
+    out_sem, in_sem,
 ):
     clips, protos, width, n_z, n_p = dims
     batch_me = lax.axis_index("batch")
@@ -91,19 +91,17 @@
         return acc
 
     def start_all(ref, me, count, ids, send, recv):
-        copies = []
         for d in range(1, count):
-            copy = remote(ref.at[me], ref.at[me], send.at[d], recv.at[d], ids(d))
-            copy.start()
-            copies.append(copy)
-        return copies
+            remote(ref.at[me], ref.at[me], send, recv, ids(d)).start()
+        others = ref.at[pl.ds(0, count - 1)]
+        return remote(others, others, send, recv, ids(1))
 
     zero = jnp.zeros((8, 128), F32)
 
     def put_cols(it, v, cols):
         for c in range(lane_chunks):
             col_z[it, v, me_z, c:c + 1, :] = jnp.sum(cols[c], axis=0, keepdims=True)
-        return start_all(col_z.at[it, v], me_z, n_z, z_id, col_send.at[it, v], col_sem.at[it, v])
+        return start_all(col_z.at[it, v], me_z, n_z, z_id, col_send, col_sem.at[it, v])
 
     def lane_sums(block):
         return jnp.sum(block.T, axis=0, keepdims=True)
@@ -113,16 +111,19 @@
             at = slice(v * clips + i * 128, v * clips + (i + 1) * 128)
             target[at, :] = jnp.broadcast_to(values[i:i + 1, :], (128, 128)).T
 
-    pending = []
     counter = [0]
 
-    def send(src, dst, device):
-        n = counter[0]
-        counter[0] += 1
-        copy = remote(src, dst, out_sem.at[n], in_sem.at[n], device)
+    def slots(n):
+        counter[0] += n
+        return counter[0] - n
+
+    def send(src, dst, device, group, slot):
+        copy = remote(src, dst, out_sem.at[group], in_sem.at[slot], device)
         copy.start()
-        pending.append(copy)
         return copy
+
+    def bytes_of(ref, group, slot):
+        return remote(ref, ref, out_sem.at[group], in_sem.at[slot], partner)
 
     def add_to(ref, value):
         ref[...] = ref[...] + value
@@ -135,13 +136,16 @@
     z_next, z_prev = z_id(1), z_id(n_z - 1)
 
     class Scatter4:
-        def __init__(self, view, me, ahead, behind, buf):
+        def __init__(self, view, me, ahead, behind, buf, group):
             self.view, self.me, self.ahead, self.behind, self.buf = view, me, ahead, behind, buf
+            self.group, self.first = group, slots(3)
             self.c = {}
 
         def send(self, slot, dest, part):
             device = self.ahead if slot < 3 else self.behind
-            self.c[slot] = send(self.view(dest, part), self.buf.at[slot], device)
+            self.c[slot] = send(
+                self.view(dest, part), self.buf.at[slot], device, self.group,
+                self.first + {0: 0, 3: 1}.get(slot, 2))
 
         def start(self):
             m = self.me
@@ -160,19 +164,21 @@
             self.send(5, (m + 3) % 4, 1)
 
         def finish(self):
-            for slot in (1, 4, 2, 5):
-                self.c[slot].wait_recv()
+            bytes_of(self.buf.at[pl.ds(0, 4)], self.group, self.first + 2).wait_recv()
             add_to(self.view(self.me, 0), self.buf[2] + self.buf[4])
             add_to(self.view(self.me, 1), self.buf[1] + self.buf[5])
 
     class Gather4:
-        def __init__(self, view, me, ahead, behind):
-            self.view, self.me, self.ahead, self.behind = view, me, ahead, behind
+        def __init__(self, view, me, ahead, behind, like, group):
+            self.view, self.me, self.ahead, self.behind, self.like = view, me, ahead, behind, like
+            self.group, self.first = group, slots(3)
             self.c = {}
 
         def send(self, slot, owner, part):
             spot = self.view(owner, part)
-            self.c[slot] = send(spot, spot, self.ahead if slot < 3 else self.behind)
+            self.c[slot] = send(
+                spot, spot, self.ahead if slot < 3 else self.behind, self.group,
+                self.first + {0: 0, 3: 1}.get(slot, 2))
 
         def start(self):
             self.send(0, self.me, 0)
@@ -187,8 +193,7 @@
             self.send(5, (self.me + 1) % 4, 1)
 
         def finish(self):
-            for slot in (1, 4, 2, 5):
-                self.c[slot].wait_recv()
+            bytes_of(self.like.at[pl.ds(0, 4)], self.group, self.first + 2).wait_recv()
 
     def quarter(half, part):
         return pl.ds(half * 64 + part * 32, 32)
@@ -223,17 +228,17 @@
 
     def scatter(ref):
         return (
-            Both(Scatter4(along_x(ref, 0), x, x_next, x_prev, rs_buf.at[0]),
-                 Scatter4(along_y(ref, 1), y, y_next, y_prev, rs_buf.at[1])),
-            Both(Scatter4(in_y(ref, 0), y, y_next, y_prev, rs_small.at[0]),
-                 Scatter4(in_x(ref, 1), x, x_next, x_prev, rs_small.at[1])))
+            Both(Scatter4(along_x(ref, 0), x, x_next, x_prev, rs_buf.at[0], 0),
+                 Scatter4(along_y(ref, 1), y, y_next, y_prev, rs_buf.at[1], 0)),
+            Both(Scatter4(in_y(ref, 0), y, y_next, y_prev, rs_small.at[0], 1),
+                 Scatter4(in_x(ref, 1), x, x_next, x_prev, rs_small.at[1], 1)))
 
     def gather(ref):
         return (
-            Both(Gather4(in_y(ref, 0), y, y_next, y_prev),
-                 Gather4(in_x(ref, 1), x, x_next, x_prev)),
-            Both(Gather4(along_x(ref, 0), x, x_next, x_prev),
-                 Gather4(along_y(ref, 1), y, y_next, y_prev)))
+            Both(Gather4(in_y(ref, 0), y, y_next, y_prev, rs_small.at[0], 2),
+                 Gather4(in_x(ref, 1), x, x_next, x_prev, rs_small.at[1], 2)),
+            Both(Gather4(along_x(ref, 0), x, x_next, x_prev, rs_buf.at[0], 3),
+                 Gather4(along_y(ref, 1), y, y_next, y_prev, rs_buf.at[1], 3)))
 
     hops = (4, 3, 3, 2, 2, 1, 1)
     split = 1
@@ -242,6 +247,7 @@
 
     class ScatterZ:
         def __init__(self):
+            self.first = slots(2 * (units - back) + 1)
             self.c = {}
 
         def view(self, dest, way, i):
@@ -255,18 +261,23 @@
                 if i >= back:
                     self.c[way, i - back].wait_recv()
                     add_to(spot, z_buf[way, i - back])
-                self.c[way, i] = send(spot, z_buf.at[way, i], z_prev if way else z_next)
+                slot = self.first + min(2 * i + way, 2 * (units - back))
+                self.c[way, i] = send(spot, z_buf.at[way, i], z_prev if way else z_next, 4, slot)
 
         def finish(self):
+            last = z_buf.at[:, pl.ds(units - back, back)]
+            bytes_of(last, 4, self.first + 2 * (units - back)).wait_recv()
             for i in range(units - back, units):
                 for way in (0, 1):
-                    self.c[way, i].wait_recv()
                     add_to(self.view(me_z, way, i), z_buf[way, i])
 
     class GatherZ:
         def __init__(self):
             self.c = {}
-            self.p = []
+            self.first, self.last = slots(2 * units), slots(1)
+
+        def pass_on(self, spot):
+            send(spot, spot, partner, 6, self.last)
 
         def view(self, owner, way, i):
             part = i // split % 2 ^ way
@@ -284,19 +295,18 @@
                     spot = self.relay(way, i - back)
                 else:
                     spot = self.view(me_z, way, i)
-                self.c[way, i] = send(spot, spot, z_prev if way else z_next)
+                self.c[way, i] = send(
+                    spot, spot, z_prev if way else z_next, 5, self.first + 2 * i + way)
                 if i >= back:
-                    self.p.append(send(spot, spot, partner))
+                    self.pass_on(spot)
 
         def own(self):
-            spot = agw.at[core * n_z + me_z]
-            self.p.append(send(spot, spot, partner))
+            self.pass_on(agw.at[core * n_z + me_z])
 
         def finish(self):
             for i in range(units - back, units):
                 for way in (0, 1):
-                    spot = self.relay(way, i)
-                    self.p.append(send(spot, spot, partner))
+                    self.pass_on(self.relay(way, i))
 
 
     step_m, step_w = 512, 512
@@ -343,22 +353,19 @@
             return carry
 
         lax.fori_loop(0, view_blocks // 2, step, 0)
-        return start_all(row_recv.at[it, v], me_p, n_p, p_id, row_send.at[it, v], row_sem.at[it, v])
+        return start_all(row_recv.at[it, v], me_p, n_p, p_id, row_send, row_sem.at[it, v])
 
     def wait_all(copies):
-        for copy in copies:
-            copy.wait_recv()
-        sends.extend(copies)
+        copies.wait_recv()
 
     def pair_start(it, v, copies):
         wait_all(copies)
         pair = col_pair.at[it, v]
         pair[core] = total_of(col_z.at[it, v], n_z)
-        copy = remote(pair.at[core], pair.at[core], colp_send.at[it, v], colp_sem.at[it, v], partner)
+        copy = remote(pair.at[core], pair.at[core], colp_send, colp_sem.at[it, v], partner)
         copy.start()
         return copy
 
-    sends = []
     z_copies = [None, None]
     row_copies = [None, None]
     z_cols = first_pass(0)
@@ -376,7 +383,7 @@
         return carry
 
     lax.fori_loop(0, row_blocks, soft_totals, 0)
-    den_copies = start_all(den_recv, me_p, n_p, p_id, den_send, den_sem)
+    den_copies = start_all(den_recv, me_p, n_p, p_id, small_send.at[0], small_sem.at[0])
 
     def transpose_unit(i, carry):
         at = pl.ds(pl.multiple_of(i * 128, 128), 128)
@@ -420,7 +427,7 @@
     for it in range(ITERS):
         pairs = [pair_start(it, v, z_copies[v]) for v in range(2)]
         for v in range(2):
-            wait_all([pairs[v]])
+            wait_all(pairs[v])
             scale[v] = 1.0 / (protos_all * (col_pair[it, v, 0] + col_pair[it, v, 1]))
             row_copies[v] = rows_pass(it, v)
         if it == 0:
@@ -452,11 +459,12 @@
         return jnp.sum(sq[:, :128] + sq[:, 128:], axis=0, keepdims=True)
 
     theirs = (1 - core) * n_z
+    pair_slot = slots(1)
 
     def pair_piece(i):
         return remote(
             dct.at[pl.ds(theirs + 2 * i, 2)], dc_pair.at[pl.ds(2 * i, 2)],
-            pair_out.at[i], pair_in.at[i], partner)
+            out_sem.at[7], in_sem.at[pair_slot], partner)
 
     def dc_dot(first_chunk, sending):
         def step(i, carry):
@@ -479,10 +487,9 @@
     r1.start()
     dc_dot(theirs, True)
     dc_dot(core * n_z, False)
-    for i in range(n_z // 2):
-        pair_piece(i).wait_recv()
-        for j in (2 * i, 2 * i + 1):
-            dc_half[j] = dct[core * n_z + j] + dc_pair[j]
+    bytes_of(dc_pair, 7, pair_slot).wait_recv()
+    for j in range(n_z):
+        dc_half[j] = dct[core * n_z + j] + dc_pair[j]
     zs.step(0)
     zs.step(1)
     r1.mid()
@@ -510,7 +517,7 @@
     sq_p[me_p, 0:1, :] = lanes_square(dw_own)
     sq_p[me_p, 1:2, :] = lanes_square(dx_own)
     sq_p[me_p, 2:8, :] = jnp.zeros((6, 128), F32)
-    sq_copies = start_all(sq_p, me_p, n_p, p_id, send_sem, sqp_sem)
+    sq_copies = start_all(sq_p, me_p, n_p, p_id, small_send.at[1], small_sem.at[1])
     g1.mid()
     zg.step(2)
     g1.finish()
@@ -518,8 +525,9 @@
     zg.step(3)
     zg.step(4)
     wait_all(sq_copies)
+    sqp_copies = sq_copies
     sq_z[batch_me] = total_of(sq_p, n_p)
-    sq_copies = start_all(sq_z, batch_me, 2 * n_z, b_id, sqz_send, sqz_sem)
+    sq_copies = start_all(sq_z, batch_me, 2 * n_z, b_id, small_send.at[2], small_sem.at[2])
     zg.step(5)
     g2.mid()
     zg.step(6)
@@ -531,12 +539,17 @@
         out[...] = jnp.broadcast_to(
             lax.rsqrt(square[i:i + 1, :] / entries[i] + NORM_EPS), (8, width))
     g2.finish()
-    for copy in zg.p:
-        copy.wait_recv()
-    for i in range(n_z // 2):
-        pair_piece(i).wait_send()
-    for copy in pending + sends:
-        copy.wait_send()
+    bytes_of(dc_pair, 6, zg.last).wait_recv()
+    for group, ref in enumerate((rs_buf, rs_small, rs_small, rs_buf, z_buf, z_buf, dc_pair, dc_pair)):
+        bytes_of(ref, group, 0).wait_send()
+    for ref, sem in (
+        (col_z.at[:, :, pl.ds(0, n_z - 1)], col_send),
+        (col_pair.at[:, :, 0], colp_send),
+        (row_recv.at[:, :, pl.ds(0, n_p - 1)], row_send),
+    ):
+        remote(ref, ref, sem, in_sem.at[0], partner).wait_send()
+    for copies in (den_copies, sqp_copies, sq_copies):
+        copies.wait_send()
 
 
 def body(slow_embed, fast_embed, prototypes):
@@ -573,11 +586,8 @@
         vmem((n_p, row_blocks, 128), F32),
         vmem((n_p, 8, 128), F32),
         vmem((n_b, 8, 128), F32),
-        DMA((16,)), DMA((ITERS, 2, n_z)), DMA((ITERS, 2, n_z)), DMA((ITERS, 2)), DMA((ITERS, 2)),
-        DMA((ITERS, 2, n_p)), DMA((ITERS, 2, n_p)),
-        DMA((n_p,)), DMA((n_p,)),
-        DMA((n_p,)), DMA((n_b,)), DMA((n_b,)), DMA((n_z // 2,)), DMA((n_z // 2,)),
-        DMA((COPIES,)), DMA((COPIES,)),
+        DMA(()), DMA((ITERS, 2)), DMA(()), DMA((ITERS, 2)), DMA(()), DMA((ITERS, 2)),
+        DMA((3,)), DMA((3,)), DMA((8,)), DMA((COPIES,)),
     ]
     whole = pl.BlockSpec(memory_space=pltpu.VMEM)
     dw, dx, dw_factor, dx_factor = pl.pallas_call(

time: 108 us -> 101 us (0.935)
  Pallas kernels: 104 us -> 97.5 us
    pallas_call x1, Pallas kernels: 104 us -> 97.5 us  [body(): pl.pallas_call(functools.partial(kernel, (clips, protos, width, n_z, n_p)...]
where the time goes in v7:
time: 101 us
  Pallas kernels  97.5 us (97%)
  other arithmetic  2.92 us (3%)
    pallas_call x1, Pallas kernels, body(): pl.pallas_call(functools.partial(kernel, (clips, protos, width, n_z, n_p)...  97.5 us
    mul x2, other arithmetic, scaled(): return (array.reshape(rows // 8, 8, width) * factor).reshape(rows, width)  2.92 us

profile of v7, /device:TPU:1, one launch (start us, length us, event | category | flops | bytes accessed | tf_op | source)
XLA Modules:
  0.0 101.2 jit_solution(5113410755366608612)
XLA Ops:
  0.6 97.5 %swav.1 = (f32[16,128,256]{2,1,0:T(8,128)S(1)}, f32[4,4,128,256]{3,2,1,0:T(8,128)S(1)}, f32[8,256]{1,0:T(8,128)S(1)}, f32[8,256]{1,0:T(8,128)S(1)}) custom-call(bf16[1024,256]{1,0:T(8,128)(2,1)} %slow_ref.1, bf16[1024,256]{1,0:T(8,128)(2,1)} %fast_ref.1, f32[2048,256]{1,0:T(8,128)} %proto_ref.1), custom_call_target="tpu_custom_call" | custom-call | tf_op jit(solution)/shard_map/swav/pallas_call | solution.py:593
  98.1 1.5 %bitcast_multiply_fusion = f32[2048,256]{1,0:T(8,128)} fusion(f32[16,128,256]{2,1,0:T(8,128)S(1)} %get-tuple-element.7, f32[8,256]{1,0:T(8,128)S(1)} %get-tuple-element.8), kind=kLoop, calls=%fused_computation | loop fusion | flops 524288 | bytes 4202496 | tf_op jit(solution)/shard_map/mul | solution.py:610
  99.6 0.1 fusion
  99.7 1.5 %bitcast_multiply_fusion.1 = (f32[1024,256]{1,0:T(8,128)}, f32[1024,256]{1,0:T(8,128)}) fusion(f32[2,4,128,256]{3,2,1,0:T(8,128)S(1)} %get-tuple-element.11, f32[8,256]{1,0:T(8,128)S(1)} %get-tuple-element.10, f32[2,4,128,256]{3,2,1,0:T(8,128)S(1)} %get-tuple-element.12), kind=kLoop, calls=%fused_computation.1 | loop fusion | flops 524288 | bytes 4202496 | tf_op jit(solution)/shard_map/mul | solution.py:610

commit v8 on v7

--- a/solution.py
+++ b/solution.py
@@ -51,7 +51,13 @@
     embeds = (slow_ref, fast_ref)
 
     def p_id(d):
-        return {"proto": (me_p + d) % n_p}
+        return {"proto": (me_p // 4 + d // 4) % 4 * 4 + (me_p + d) % 4}
+
+    def p_hops(d):
+        return min(d // 4, 4 - d // 4) + min(d % 4, 4 - d % 4)
+
+    def z_hops(d):
+        return min(d, n_z - d)
 
     def z_id(d):
         return {"batch": ((me_z + d) % n_z) * 2 + core}
@@ -91,7 +97,8 @@
         return acc
 
     def start_all(ref, me, count, ids, send, recv):
-        for d in range(1, count):
+        hops_to = {p_id: p_hops, z_id: z_hops}.get(ids, lambda d: z_hops(d // 2))
+        for d in sorted(range(1, count), key=hops_to, reverse=True):
             remote(ref.at[me], ref.at[me], send, recv, ids(d)).start()
         others = ref.at[pl.ds(0, count - 1)]
         return remote(others, others, send, recv, ids(1))

time: 101 us -> 98.1 us (0.971)
  Pallas kernels: 97.5 us -> 94.3 us
    pallas_call x1, Pallas kernels: 97.5 us -> 94.3 us  [body(): pl.pallas_call(functools.partial(kernel, (clips, protos, width, n_z, n_p)...]
where the time goes in v8:
time: 98.1 us; the launch traced here: 98 us
  Pallas kernels  94.3 us (96%)
  other arithmetic  2.92 us (3%)
    pallas_call x1, Pallas kernels, body(): pl.pallas_call(functools.partial(kernel, (clips, protos, width, n_z, n_p)...  94.3 us
    mul x2, other arithmetic, scaled(): return (array.reshape(rows // 8, 8, width) * factor).reshape(rows, width)  2.92 us

profile of v8, /device:TPU:1, one launch (start us, length us, event | category | flops | bytes accessed | tf_op | source)
XLA Modules:
  0.0 98.0 jit_solution(17594405624017038634)
XLA Ops:
  0.6 94.3 %swav.1 = (f32[16,128,256]{2,1,0:T(8,128)S(1)}, f32[4,4,128,256]{3,2,1,0:T(8,128)S(1)}, f32[8,256]{1,0:T(8,128)S(1)}, f32[8,256]{1,0:T(8,128)S(1)}) custom-call(bf16[1024,256]{1,0:T(8,128)(2,1)} %slow_ref.1, bf16[1024,256]{1,0:T(8,128)(2,1)} %fast_ref.1, f32[2048,256]{1,0:T(8,128)} %proto_ref.1), custom_call_target="tpu_custom_call" | custom-call | tf_op jit(solution)/shard_map/swav/pallas_call | solution.py:600
  94.9 1.5 %bitcast_multiply_fusion = f32[2048,256]{1,0:T(8,128)} fusion(f32[16,128,256]{2,1,0:T(8,128)S(1)} %get-tuple-element.7, f32[8,256]{1,0:T(8,128)S(1)} %get-tuple-element.8), kind=kLoop, calls=%fused_computation | loop fusion | flops 524288 | bytes 4202496 | tf_op jit(solution)/shard_map/mul | solution.py:617
  96.4 0.1 fusion
  96.5 1.5 %bitcast_multiply_fusion.1 = (f32[1024,256]{1,0:T(8,128)}, f32[1024,256]{1,0:T(8,128)}) fusion(f32[2,4,128,256]{3,2,1,0:T(8,128)S(1)} %get-tuple-element.11, f32[8,256]{1,0:T(8,128)S(1)} %get-tuple-element.10, f32[2,4,128,256]{3,2,1,0:T(8,128)S(1)} %get-tuple-element.12), kind=kLoop, calls=%fused_computation.1 | loop fusion | flops 524288 | bytes 4202496 | tf_op jit(solution)/shard_map/mul | solution.py:617

commit v9 on v8

--- a/solution.py
+++ b/solution.py
@@ -80,12 +80,12 @@
         pl.semaphore_signal(barrier, inc=1, device_id=b_id(d), device_id_type=MESH)
 
     def proto_norm(i, carry):
-        at = pl.ds(pl.multiple_of(i * 128, 128), 128)
+        at = pl.ds(pl.multiple_of(i * 512, 512), 512)
         unit, _ = normalized(proto_ref[at, :])
         proto_b[at, :] = unit.astype(BF16)
         return carry
 
-    lax.fori_loop(0, protos // 128, proto_norm, 0)
+    lax.fori_loop(0, protos // 512, proto_norm, 0)
 
     def chunk(c):
         return slice(c * 128, (c + 1) * 128)
@@ -506,8 +506,8 @@
     r1.finish()
     r2.start()
     zs.step(5)
+    r2.mid()
     zs.step(6)
-    r2.mid()
     r2.finish()
     at = pl.ds(pl.multiple_of((me_p % view_blocks) * 128, 128), 128)
     raw = jnp.where(me_p < view_blocks, slow_ref[at, :].astype(F32), fast_ref[at, :].astype(F32))
@@ -526,9 +526,9 @@
     sq_p[me_p, 2:8, :] = jnp.zeros((6, 128), F32)
     sq_copies = start_all(sq_p, me_p, n_p, p_id, small_send.at[1], small_sem.at[1])
     g1.mid()
-    zg.step(2)
     g1.finish()
     g2.start()
+    zg.step(2)
     zg.step(3)
     zg.step(4)
     wait_all(sq_copies)

time: 98.1 us -> 100 us (1.019)
  Pallas kernels: 94.3 us -> 96.3 us
    pallas_call x1, Pallas kernels: 94.3 us -> 96.3 us  [body(): pl.pallas_call(functools.partial(kernel, (clips, protos, width, n_z, n_p)...]
where the time goes in v9:
time: 100 us
  Pallas kernels  96.3 us (96%)
  other arithmetic  2.92 us (3%)
    pallas_call x1, Pallas kernels, body(): pl.pallas_call(functools.partial(kernel, (clips, protos, width, n_z, n_p)...  96.3 us
    mul x2, other arithmetic, scaled(): return (array.reshape(rows // 8, 8, width) * factor).reshape(rows, width)  2.92 us

profile of v9, /device:TPU:1, one launch (start us, length us, event | category | flops | bytes accessed | tf_op | source)
XLA Modules:
  0.0 100.0 jit_solution(9725092159813322766)
XLA Ops:
  0.6 96.3 %swav.1 = (f32[16,128,256]{2,1,0:T(8,128)S(1)}, f32[4,4,128,256]{3,2,1,0:T(8,128)S(1)}, f32[8,256]{1,0:T(8,128)S(1)}, f32[8,256]{1,0:T(8,128)S(1)}) custom-call(bf16[1024,256]{1,0:T(8,128)(2,1)} %slow_ref.1, bf16[1024,256]{1,0:T(8,128)(2,1)} %fast_ref.1, f32[2048,256]{1,0:T(8,128)} %proto_ref.1), custom_call_target="tpu_custom_call" | custom-call | tf_op jit(solution)/shard_map/swav/pallas_call | solution.py:600
  97.0 1.5 %bitcast_multiply_fusion = f32[2048,256]{1,0:T(8,128)} fusion(f32[16,128,256]{2,1,0:T(8,128)S(1)} %get-tuple-element.7, f32[8,256]{1,0:T(8,128)S(1)} %get-tuple-element.8), kind=kLoop, calls=%fused_computation | loop fusion | flops 524288 | bytes 4202496 | tf_op jit(solution)/shard_map/mul | solution.py:617
  98.4 0.1 fusion
  98.6 1.5 %bitcast_multiply_fusion.1 = (f32[1024,256]{1,0:T(8,128)}, f32[1024,256]{1,0:T(8,128)}) fusion(f32[2,4,128,256]{3,2,1,0:T(8,128)S(1)} %get-tuple-element.11, f32[8,256]{1,0:T(8,128)S(1)} %get-tuple-element.10, f32[2,4,128,256]{3,2,1,0:T(8,128)S(1)} %get-tuple-element.12), kind=kLoop, calls=%fused_computation.1 | loop fusion | flops 524288 | bytes 4202496 | tf_op jit(solution)/shard_map/mul | solution.py:617

commit v10 on v9

--- a/solution.py
+++ b/solution.py
@@ -503,11 +503,11 @@
     zs.step(2)
     zs.step(3)
     zs.step(4)
+    zs.step(5)
     r1.finish()
     r2.start()
-    zs.step(5)
+    zs.step(6)
     r2.mid()
-    zs.step(6)
     r2.finish()
     at = pl.ds(pl.multiple_of((me_p % view_blocks) * 128, 128), 128)
     raw = jnp.where(me_p < view_blocks, slow_ref[at, :].astype(F32), fast_ref[at, :].astype(F32))
@@ -526,9 +526,9 @@
     sq_p[me_p, 2:8, :] = jnp.zeros((6, 128), F32)
     sq_copies = start_all(sq_p, me_p, n_p, p_id, small_send.at[1], small_sem.at[1])
     g1.mid()
+    zg.step(2)
     g1.finish()
     g2.start()
-    zg.step(2)
     zg.step(3)
     zg.step(4)
     wait_all(sq_copies)

time: 100 us -> 99.4 us (level)
  no operation moved by 1% of the time
where the time goes in v10:
time: 99.4 us; the launch traced here: 99.3 us
  Pallas kernels  95.6 us (96%)
  other arithmetic  2.92 us (3%)
    pallas_call x1, Pallas kernels, body(): pl.pallas_call(functools.partial(kernel, (clips, protos, width, n_z, n_p)...  95.6 us
    mul x2, other arithmetic, scaled(): return (array.reshape(rows // 8, 8, width) * factor).reshape(rows, width)  2.92 us

profile of v10, /device:TPU:1, one launch (start us, length us, event | category | flops | bytes accessed | tf_op | source)
XLA Modules:
  0.0 99.3 jit_solution(15244154691750313795)
XLA Ops:
  0.6 95.6 %swav.1 = (f32[16,128,256]{2,1,0:T(8,128)S(1)}, f32[4,4,128,256]{3,2,1,0:T(8,128)S(1)}, f32[8,256]{1,0:T(8,128)S(1)}, f32[8,256]{1,0:T(8,128)S(1)}) custom-call(bf16[1024,256]{1,0:T(8,128)(2,1)} %slow_ref.1, bf16[1024,256]{1,0:T(8,128)(2,1)} %fast_ref.1, f32[2048,256]{1,0:T(8,128)} %proto_ref.1), custom_call_target="tpu_custom_call" | custom-call | tf_op jit(solution)/shard_map/swav/pallas_call | solution.py:600
  96.2 1.5 %bitcast_multiply_fusion = f32[2048,256]{1,0:T(8,128)} fusion(f32[16,128,256]{2,1,0:T(8,128)S(1)} %get-tuple-element.7, f32[8,256]{1,0:T(8,128)S(1)} %get-tuple-element.8), kind=kLoop, calls=%fused_computation | loop fusion | flops 524288 | bytes 4202496 | tf_op jit(solution)/shard_map/mul | solution.py:617
  97.7 0.1 fusion
  97.8 1.5 %bitcast_multiply_fusion.1 = (f32[1024,256]{1,0:T(8,128)}, f32[1024,256]{1,0:T(8,128)}) fusion(f32[2,4,128,256]{3,2,1,0:T(8,128)S(1)} %get-tuple-element.11, f32[8,256]{1,0:T(8,128)S(1)} %get-tuple-element.10, f32[2,4,128,256]{3,2,1,0:T(8,128)S(1)} %get-tuple-element.12), kind=kLoop, calls=%fused_computation.1 | loop fusion | flops 524288 | bytes 4202496 | tf_op jit(solution)/shard_map/mul | solution.py:617
